TPU v7x, 32 devices: a whole 2x2x4 slice. The times are simulated.
32 devices in a mesh: batch: 8 (over y, x, core), chan: 4 (over z).
Axes of the slice: x: 2, y: 2, z: 4, core: 2. Of those that a mesh axis runs over, the one named last changes fastest.
Arguments:
- fine_inputs: bfloat16 [8, 32, 32, 512], P('batch'), may hold values from -6 to 6
- fine_upstream: bfloat16 [8, 32, 32, 512], P('batch', None, None, 'chan'), may hold values from -6 to 6
- fine_bank: bfloat16 [8, 9, 512, 512], P(None, None, 'batch', 'chan'), may hold values from -0.09375 to 0.09375
- fine_coefs: float32 [8, 8], replicated, may hold values from 0 to 1, as said below
- coarse_inputs: bfloat16 [8, 16, 16, 512], P('batch'), may hold values from -6 to 6
- coarse_upstream: bfloat16 [8, 16, 16, 512], P('batch', None, None, 'chan'), may hold values from -6 to 6
- coarse_bank: bfloat16 [8, 9, 512, 512], P(None, None, 'batch', 'chan'), may hold values from -0.09375 to 0.09375
- coarse_coefs: float32 [8, 8], replicated, may hold values from 0 to 1, as said below
Outputs:
- fine_delta: bfloat16 [8, 32, 32, 512], P('batch', None, None, 'chan')
- fine_update: float32 [8, 9, 512, 512], P(None, None, 'batch', 'chan')
- fine_logit: float32 [8, 8], P('batch')
- coarse_delta: bfloat16 [8, 16, 16, 512], P('batch', None, None, 'chan')
- coarse_update: float32 [8, 9, 512, 512], P(None, None, 'batch', 'chan')
- coarse_logit: float32 [8, 8], P('batch')
Inputs may be any that keep to these rules, and one draw needn't show every extreme that they name: Each row of fine_coefs is a softmax: positive entries that sum to one. Each row of coarse_coefs is a softmax: positive entries that sum to one.
All inputs are finite; a program needn't handle non-finite values.
Results may differ from a plain program's by a relative error of at most 0.01.
Values may be sent and summed in bfloat16 or wider, within the bound.
No kernel may reach another device: no remote copies, remote signals or barrier semaphores. Data moves between devices by JAX's collectives and lax.ppermute only.
A program may use at most 128 MiB of HBM per device.

v0:
```python
import functools

import jax
import jax.numpy as jnp
from jax import lax
from jax.experimental import pallas as pl
from jax.experimental.pallas import tpu as pltpu
from jax.sharding import PartitionSpec as P


HIGH = lax.Precision.HIGHEST
F32 = jnp.float32
BF16 = jnp.bfloat16


def shifted(padded, row_shift, col_shift, side):
    window = padded[:, row_shift : row_shift + side, col_shift : col_shift + side, :]
    return window.reshape(window.shape[0], side * side, window.shape[3])


def local_grads(inputs, upstream, kernels, side):
    samples_here = inputs.shape[0]
    pad_in = jnp.pad(inputs, ((0, 0), (1, 1), (1, 1), (0, 0)))
    pad_up = jnp.pad(upstream, ((0, 0), (1, 1), (1, 1), (0, 0)))
    flat_up = upstream.reshape(samples_here, side * side, upstream.shape[3])
    delta = jnp.zeros((samples_here, side * side, inputs.shape[3]), F32)
    grad_taps = []
    for row_shift in range(3):
        for col_shift in range(3):
            tap = 3 * row_shift + col_shift
            window_in = shifted(pad_in, row_shift, col_shift, side)
            window_up = shifted(pad_up, 2 - row_shift, 2 - col_shift, side)
            grad_taps.append(
                jnp.einsum("bpc,bpo->bco", window_in, flat_up, preferred_element_type=F32) / side
            )
            delta = delta + jnp.einsum(
                "bpo,bco->bpc", window_up, kernels[:, tap], preferred_element_type=F32
            )
    return (delta.reshape(samples_here, side, side, inputs.shape[3]), jnp.stack(grad_taps, axis=1))


def plain_layer(inputs, upstream, bank_part, coefs):
    side = inputs.shape[1]
    flat_bank = bank_part.reshape(bank_part.shape[0], -1).astype(F32)
    mixed_all = jnp.dot(coefs, flat_bank, precision=HIGH)
    mixed_all = mixed_all.reshape((coefs.shape[0],) + bank_part.shape[1:]).astype(BF16)
    kernels = lax.all_to_all(mixed_all, "batch", split_axis=0, concat_axis=2, tiled=True)
    delta, kernel_grad = local_grads(inputs, upstream, kernels, side)
    delta_total = lax.psum(delta.astype(BF16), "chan").astype(F32)
    width = delta.shape[3] // lax.axis_size("chan")
    delta_part = lax.dynamic_slice_in_dim(delta_total, lax.axis_index("chan") * width, width, 3)
    moved = lax.all_to_all(
        kernel_grad.astype(BF16), "batch", split_axis=2, concat_axis=0, tiled=True
    ).astype(kernel_grad.dtype)
    flat_grads = moved.reshape(moved.shape[0], -1)
    update = jnp.dot(coefs.T, flat_grads, precision=HIGH).reshape(bank_part.shape)
    dcoef_part = lax.dot_general(flat_grads, flat_bank, (((1,), (1,)), ((), ())), precision=HIGH)
    return (delta_part.astype(BF16), update, dcoef_part)


def plain_logits(coefs, totals, samples_here):
    first_row = lax.axis_index("batch") * samples_here
    own_coefs = lax.dynamic_slice_in_dim(coefs, first_row, samples_here, 0)
    own_totals = lax.dynamic_slice_in_dim(totals, first_row, samples_here, 0)
    return own_coefs * (own_totals - jnp.sum(own_coefs * own_totals, axis=1, keepdims=True))


def plain_device(fi, fu, fb, fc, ci, cu, cb, cc):
    fine_delta, fine_update, fine_partial = plain_layer(fi, fu, fb, fc)
    coarse_delta, coarse_update, coarse_partial = plain_layer(ci, cu, cb, cc)
    fine_total, coarse_total = lax.psum((fine_partial, coarse_partial), ("batch", "chan"))
    fine_logit = plain_logits(fc, fine_total, fi.shape[0])
    coarse_logit = plain_logits(cc, coarse_total, fi.shape[0])
    return (fine_delta, fine_update, fine_logit, coarse_delta, coarse_update, coarse_logit)


def place():
    me = lax.axis_index("batch")
    return me, lax.div(me, 2), lax.rem(me, 2), lax.axis_index("chan")


def smem(n):
    return [pl.BlockSpec(memory_space=pltpu.SMEM) for _ in range(n)]


def hbm(n):
    return [pl.BlockSpec(memory_space=pl.ANY) for _ in range(n)]


def vmem(n):
    return [pl.BlockSpec(memory_space=pltpu.VMEM) for _ in range(n)]


def call(body, out_shapes, in_specs, out_specs, scratch=(), flops=0, nbytes=0, alone=False, grant=16 * 1024 * 1024):
    return pl.pallas_call(
        body,
        out_shape=out_shapes,
        in_specs=in_specs,
        out_specs=out_specs,
        scratch_shapes=list(scratch),
        compiler_params=pltpu.CompilerParams(vmem_limit_bytes=None if alone else grant),
        cost_estimate=pl.CostEstimate(flops=flops, bytes_accessed=nbytes, transcendentals=0),
    )


def start(src, dst, sem):
    copy = pltpu.make_async_copy(src, dst, sem)
    copy.start()
    return copy


def fill_windows(up, side, ref):
    pixels, width = up.shape
    wide = up.astype(F32)
    col = lax.rem(lax.broadcasted_iota(jnp.int32, (pixels, width), 0), side)
    zeros = jnp.zeros((side, 3 * width), BF16)
    ref[0:side, :] = zeros
    ref[side + pixels :, :] = zeros
    body = slice(side, side + pixels)
    ref[body, 0:width] = jnp.where(col == side - 1, 0.0, pltpu.roll(wide, pixels - 1, 0)).astype(BF16)
    ref[body, width : 2 * width] = up
    ref[body, 2 * width :] = jnp.where(col == 0, 0.0, pltpu.roll(wide, 1, 0)).astype(BF16)


def window(ref, side, dy):
    first = (2 - dy) * side
    return ref[first : first + ref.shape[0] - 2 * side, :]


def all_windows(ref, side):
    return jnp.concatenate([window(ref, side, dy) for dy in range(3)], axis=1)


def dot_nt(a, b):
    return lax.dot_general(a, b, (((1,), (1,)), ((), ())), preferred_element_type=F32)


def dot_tn(a, b):
    return lax.dot_general(a, b, (((0,), (0,)), ((), ())), preferred_element_type=F32)


def front_body(pairs, side, fx, fup, *rest):
    outs, (v_fx, v_fup, windows, staged, sem_in, sem_out) = rest[:pairs], rest[pairs:]
    _, pair, _, _ = place()
    loads = [start(fup, v_fup, sem_in.at[0]), start(fx, v_fx, sem_in.at[1])]
    loads[0].wait()
    fill_windows(v_fup[...], side, windows)
    loads[1].wait()
    got = dot_tn(v_fx[...], all_windows(windows, side))
    staged[...] = (got * (1.0 / side)).astype(BF16)
    rows = staged.shape[0] // pairs
    stores = []
    for d, out in enumerate(outs):
        first = pl.multiple_of(jnp.bitwise_xor(pair, d) * rows, rows)
        stores.append(start(staged.at[pl.ds(first, rows), :], out, sem_out.at[d]))
    for store in stores:
        store.wait()


def load_banks(own, other, v_banks, sems):
    taps, width = own.shape[1], own.shape[3]
    loads = []
    for t in range(taps):
        lanes = slice(t * width, (t + 1) * width)
        loads.append(
            [
                start(bank.at[:, t], v_banks.at[src, :, :, lanes], sems.at[src, t])
                for src, bank in enumerate((own, other))
            ]
        )
    return loads


def half_row(src, rows):
    _, _, half, _ = place()
    return pl.multiple_of((half if src == 0 else 1 - half) * rows, rows)


def spread(weights, chunk):
    count, terms = len(weights), len(weights[0])
    dims = (chunk, terms * chunk)
    lane = lax.broadcasted_iota(jnp.int32, dims, 1)
    same = lax.broadcasted_iota(jnp.int32, dims, 0) == lax.rem(lane, chunk)
    term = lax.div(lane[0:8], chunk)
    high, low = [], []
    for n in range(count):
        line = jnp.full((8, terms * chunk), weights[n][0], F32)
        for k in range(1, terms):
            line = jnp.where(term == k, weights[n][k], line)
        value = jnp.where(same, jnp.concatenate([line] * (chunk // 8), axis=0), 0.0)
        rounded = value.astype(BF16)
        high.append(rounded)
        low.append((value - rounded.astype(F32)).astype(BF16))
    return jnp.concatenate(high + low, axis=0)


def dot_nn(a, b):
    return lax.dot_general(a, b, (((1,), (0,)), ((), ())), preferred_element_type=F32)


def chunk_of(rows, terms):
    return max(16, min(rows, 256 // terms))


def mix_weights(pairs, coefs):
    me, _, _, _ = place()
    banks = coefs.shape[1]
    return [[coefs[jnp.bitwise_xor(me, 2 * d), k] for k in range(banks)] for d in range(pairs)]


def pack_body(pairs, cx, cup, *rest):
    packs, (v_x, v_up, sem_in, sem_out) = rest[:pairs], rest[pairs:]
    _, pair, _, _ = place()
    pixels, width = v_up.shape
    loads = [start(cup, v_up, sem_in.at[0]), start(cx, v_x, sem_in.at[1])]
    loads[0].wait()
    stores = [start(v_up, out.at[0:pixels, :], sem_out.at[0, d]) for d, out in enumerate(packs)]
    loads[1].wait()
    for d, out in enumerate(packs):
        first = pl.multiple_of(jnp.bitwise_xor(pair, d) * width, width)
        stores.append(start(v_x.at[:, pl.ds(first, width)], out.at[pixels:, :], sem_out.at[1, d]))
    for store in stores:
        store.wait()


def tables_body(pairs, chunk, fine_coefs, coarse_coefs, *tables):
    me, _, _, _ = place()
    samples = 2 * pairs
    for n, coefs in enumerate((fine_coefs, coarse_coefs)):
        banks = coefs.shape[1]
        to_updates, row = tables[2 * n : 2 * n + 2]
        weights = [[coefs[jnp.bitwise_xor(me, d), k] for d in range(samples)] for k in range(banks)]
        to_updates[...] = spread(weights, chunk)
        lane = lax.broadcasted_iota(jnp.int32, row.shape, 1)
        line = jnp.zeros(row.shape, F32)
        for k in range(banks):
            line = jnp.where(lane == k, coefs[me, k], line)
        row[...] = line


def mix_lanes(pairs, table, v_banks, staged, lanes):
    _, banks, rows, _ = v_banks.shape
    chunk = table.shape[1] // banks
    for src in range(2):
        base = half_row(src, rows)
        for at in range(0, rows, chunk):
            right = v_banks[src, :, at : at + chunk, lanes]
            got = dot_nn(table, right.reshape(banks * chunk, right.shape[2]))
            got = (got[: pairs * chunk] + got[pairs * chunk :]).astype(BF16)
            into = pl.ds(pl.multiple_of(base + at, 16), chunk)
            for d in range(pairs):
                staged[d, into, lanes] = got[d * chunk : (d + 1) * chunk]


def mix_body(pairs, coefs, own, other, *rest):
    outs, (s_coefs, v_banks, staged, sem_coefs, sem_in, sem_out) = rest[:pairs], rest[pairs:]
    taps, width = own.shape[1], own.shape[3]
    first = start(coefs, s_coefs, sem_coefs)
    loads = load_banks(own, other, v_banks, sem_in)
    first.wait()
    table = spread(mix_weights(pairs, s_coefs), chunk_of(own.shape[2], own.shape[0]))
    stores = []
    for t in range(0, taps, 3):
        for some in loads[t : t + 3]:
            for load in some:
                load.wait()
        lanes = slice(t * width, (t + 3) * width)
        mix_lanes(pairs, table, v_banks, staged, lanes)
        for d, out in enumerate(outs):
            stores.append(start(staged.at[d, :, lanes], out.at[:, lanes], sem_out.at[d, t]))
    for store in stores:
        store.wait()


def delta_body(pairs, side, up, *rest):
    mixed, outs = rest[:pairs], rest[pairs : 2 * pairs]
    v_up, windows, kernels, staged, sem_in, sem_out = rest[2 * pairs :]
    _, pair, _, chan = place()
    rows = kernels.shape[0] // pairs
    first_load = start(up, v_up, sem_in.at[pairs])
    loads = []
    for d in range(pairs):
        slot = jnp.bitwise_xor(jnp.bitwise_xor(pair, d), chan)
        at = pl.multiple_of(slot * rows, rows)
        loads.append(start(mixed[d], kernels.at[pl.ds(at, rows), :], sem_in.at[d]))
    first_load.wait()
    fill_windows(v_up[...], side, windows)
    for load in loads:
        load.wait()
    stores = []
    got = dot_nt(all_windows(windows, side), kernels[...])
    for slot in range(pairs):
        staged[slot] = got[:, slot * rows : (slot + 1) * rows].astype(BF16)
        stores.append(start(staged.at[slot], outs[slot], sem_out.at[slot]))
    for store in stores:
        store.wait()


def dcoef_rows(pairs, grads, v_banks, lane0):
    _, banks, rows, span = v_banks.shape
    chunk = chunk_of(rows, banks)
    cross = None
    for src in range(2):
        for at in range(0, rows, chunk):
            first = pl.multiple_of(half_row(src, rows) + at, 16)
            left = grads[:, pl.ds(first, chunk), :].reshape(pairs * chunk, span)
            right = v_banks[src, :, at : at + chunk, :].reshape(banks * chunk, span)
            one = dot_nt(left, right)
            cross = one if cross is None else cross + one
    row = lax.rem(lax.broadcasted_iota(jnp.int32, cross.shape, 0), chunk)
    col = lax.rem(lax.broadcasted_iota(jnp.int32, cross.shape, 1), chunk)
    kept = jnp.where(row == col, cross, 0.0)
    kept = jnp.sum(kept.reshape(pairs, chunk, banks * chunk), axis=1)
    bank_of = lax.div(lax.broadcasted_iota(jnp.int32, kept.shape, 1), chunk)
    lane = lax.broadcasted_iota(jnp.int32, (pairs, 128), 1)
    total = jnp.zeros((pairs, 128), F32)
    for k in range(banks):
        one = jnp.sum(jnp.where(bank_of == k, kept, 0.0), axis=1, keepdims=True)
        total = jnp.where(lane == lane0 + k, one, total)
    return total


def coarse_body(pairs, side, coefs, own, other, *rest):
    ups, parts, rest = rest[:pairs], rest[pairs : 2 * pairs], rest[2 * pairs :]
    s_coefs, v_banks, v_mixed, v_ups, windows, v_parts, sem_coefs, sem_bank, sem_in, sem_out = rest
    taps, width = own.shape[1], own.shape[3]
    pixels = side * side
    first = start(coefs, s_coefs, sem_coefs)
    loads = [start(ups[d].at[0:pixels, :], v_ups.at[d], sem_in.at[d]) for d in range(pairs)]
    bank_loads = load_banks(own, other, v_banks, sem_bank)
    first.wait()
    table = spread(mix_weights(pairs, s_coefs), chunk_of(own.shape[2], own.shape[0]))
    for t in range(0, taps, 3):
        for some in bank_loads[t : t + 3]:
            for load in some:
                load.wait()
        mix_lanes(pairs, table, v_banks, v_mixed, slice(t * width, (t + 3) * width))
    stores = []
    third = windows.shape[1]
    for d in range(pairs):
        loads[d].wait()
        fill_windows(v_ups[d], side, windows)
        part = None
        for dy in range(3):
            one = dot_nt(window(windows, side, dy), v_mixed[d, :, dy * third : (dy + 1) * third])
            part = one if part is None else part + one
        v_parts[d] = part.astype(BF16)
        stores.append(start(v_parts.at[d], parts[d], sem_out.at[d]))
    for store in stores:
        store.wait()


def calm_body(pairs, side, own, other, *rest):
    bufs, grads, table, rest = rest[:pairs], rest[pairs : 2 * pairs], rest[2 * pairs], rest[2 * pairs + 1 :]
    v_banks, v_bufs, windows, v_grads, sem_bank, sem_in, sem_out = rest
    pixels = side * side
    loads = [start(bufs[d], v_bufs.at[d], sem_in.at[d]) for d in range(pairs)]
    bank_loads = load_banks(own, other, v_banks, sem_bank)
    stores = []
    for d in range(pairs):
        loads[d].wait()
        fill_windows(v_bufs[d, 0:pixels, :], side, windows)
        got = dot_tn(v_bufs[d, pixels:, :], all_windows(windows, side))
        v_grads[d] = (got * (1.0 / side)).astype(BF16)
        stores.append(start(v_grads.at[d], grads[d], sem_out.at[d]))
    for some in bank_loads:
        for load in some:
            load.wait()
    table[...] = dcoef_rows(pairs, v_grads, v_banks, own.shape[0])
    for store in stores:
        store.wait()


def as_pair(rows):
    high = rows.astype(BF16)
    return jnp.concatenate([high, (rows - high.astype(F32)).astype(BF16)], axis=0)


def from_pair(both):
    wide = both.astype(F32)
    return wide[0:8] + wide[8:16]


def late_body(pairs, own, other, more, *rest):
    gots, parts, outs = rest[:pairs], rest[pairs : 2 * pairs - 1], rest[2 * pairs - 1 : 3 * pairs - 2]
    mine, v_banks, v_gots, v_out, sem_bank, sem_in, sem_part, sem_out = rest[3 * pairs - 2 :]
    loads = [[start(gots[d], v_gots.at[d], sem_in.at[d]) for d in range(pairs)]]
    loads += load_banks(own, other, v_banks, sem_bank)
    pixels = parts[0].shape[0]
    loads.append(
        [start(parts[d], v_out.at[d, 0:pixels, :], sem_part.at[d]) for d in range(pairs - 1)]
    )
    for some in loads:
        for load in some:
            load.wait()
    total = dcoef_rows(pairs, v_gots, v_banks, 0) + more[...]
    mine[...] = jnp.broadcast_to(total[0:1], mine.shape)
    stores = []
    for d in range(pairs - 1):
        v_out[d, pixels:, :] = as_pair(jnp.broadcast_to(total[d + 1 : d + 2], mine.shape))
        stores.append(start(v_out.at[d], outs[d], sem_out.at[d]))
    for store in stores:
        store.wait()


def slot_body(pairs, first_part, first_row, *rest):
    gots, slots, rest = rest[: pairs - 1], rest[pairs - 1 : 2 * pairs - 1], rest[2 * pairs - 1 :]
    mine, v_slots, sem_in, sem_out = rest
    _, pair, _, chan = place()
    pixels = first_part.shape[0]
    loads, at = [], []
    for d in range(pairs):
        slot = jnp.bitwise_xor(jnp.bitwise_xor(pair, d), chan)
        at.append(slot)
        if d == 0:
            loads.append(start(first_part, v_slots.at[slot, 0:pixels, :], sem_in.at[0]))
        else:
            loads.append(start(gots[d - 1], v_slots.at[slot], sem_in.at[d]))
    for load in loads:
        load.wait()
    total = first_row[...]
    for d in range(1, pairs):
        total = total + from_pair(v_slots[at[d], pixels:, :])
    both = as_pair(total)
    mine[...] = from_pair(both)
    for s in range(pairs):
        v_slots[s, pixels:, :] = both
    stores = [start(v_slots.at[s], slots[s], sem_out.at[s]) for s in range(pairs)]
    for store in stores:
        store.wait()


def update_body(pairs, layers, *rest):
    samples = 2 * pairs
    tables, rest = rest[:layers], rest[layers:]
    all_gots, rest = rest[: layers * samples], rest[layers * samples :]
    updates, (v_grads, staged, sem_in, sem_out) = rest[:layers], rest[layers:]
    _, _, half, _ = place()
    banks, taps, rows, width = updates[0].shape
    first = pl.multiple_of(half * rows, rows)
    loads = []
    for n in range(layers):
        gots = all_gots[n * samples : (n + 1) * samples]
        for d in range(samples):
            src = gots[d % 2 * pairs + d // 2].at[pl.ds(first, rows), 0 : taps * width]
            loads.append(start(src, v_grads.at[n, d], sem_in.at[n, d]))
    for load in loads:
        load.wait()
    chunk = chunk_of(rows, samples)
    stores = []
    for n in range(layers):
        table = tables[n][...]
        half_table = banks * chunk
        for at in range(0, rows, chunk):
            right = v_grads[n, :, at : at + chunk, :].reshape(samples * chunk, taps * width)
            got = dot_nn(table, right)
            got = got[:half_table] + got[half_table:]
            for k in range(banks):
                for t in range(taps):
                    staged[n, k, t, at : at + chunk, :] = got[
                        k * chunk : (k + 1) * chunk, t * width : (t + 1) * width
                    ]
            some = slice(at, at + chunk)
            stores.append(
                start(staged.at[n, :, :, some], updates[n].at[:, :, some], sem_out.at[n, at // chunk])
            )
    for store in stores:
        store.wait()


def final_body(pairs, banks, mine, fine_row, coarse_row, *rest):
    pieces, rest = rest[: 2 * pairs], rest[2 * pairs :]
    fine_out, coarse_out, fine_delta, coarse_delta, v_fine, v_coarse, sem_in, sem_out = rest
    layers = ((v_fine, fine_delta), (v_coarse, coarse_delta))
    loads = [
        [
            start(pieces[n * pairs + d], v.at[d], sem_in.at[n, d])
            for d in range(pairs)
        ]
        for n, (v, _) in enumerate(layers)
    ]
    stores = []
    for n, (v, out) in enumerate(layers):
        for load in loads[n]:
            load.wait()
        pixels = out.shape[0]
        total = v[0, 0:pixels, :].astype(F32)
        for d in range(1, pairs):
            total = total + v[d, 0:pixels, :].astype(F32)
        v[pairs, 0:pixels, :] = total.astype(BF16)
        stores.append(start(v.at[pairs, 0:pixels, :], out, sem_out.at[n]))
    total = mine[...]
    for d in range(1, pairs):
        total = total + from_pair(v_coarse[d, pixels:, :])
    for lane0, row, out in ((0, fine_row, fine_out), (banks, coarse_row, coarse_out)):
        own = row[:, 0:banks]
        some = total[0:1, lane0 : lane0 + banks]
        out[...] = own * (some - jnp.sum(own * some, axis=1, keepdims=True))
    for store in stores:
        store.wait()


def shape(*dims, dtype=BF16):
    return jax.ShapeDtypeStruct(dims, dtype)


def pair_device(fi, fu, fb, fc, ci, cu, cb, cc):
    return pair_steps(fi, fu, fb, fc, ci, cu, cb, cc)


def pair_steps(fi, fu, fb, fc, ci, cu, cb, cc):
    pairs = lax.axis_size("chan")
    count = lax.axis_size("batch")
    fine_side, coarse_side = fi.shape[1], ci.shape[1]
    fine_px, coarse_px = fine_side**2, coarse_side**2
    channels = fi.shape[3]
    banks, taps, rows, width = fb.shape
    block = 2 * rows
    span = taps * width
    fx, fup = fi.reshape(fine_px, channels), fu.reshape(fine_px, width)
    cx, cup = ci.reshape(coarse_px, channels), cu.reshape(coarse_px, width)

    def over_batch(x, d):
        return lax.ppermute(x, "batch", [(i, i ^ d) for i in range(count)])

    def over_chan(x, d):
        return lax.ppermute(x, "chan", [(i, i ^ d) for i in range(pairs)])

    def send(move, pieces, distances):
        out = []
        for piece, d in zip(pieces, distances):
            out.append(move(piece, d))
        return out

    def to_pairs(pieces):
        moved = send(lambda x, d: over_batch(x, 2 * d), pieces[1:], range(1, pairs))
        return [pieces[0]] + moved

    dma = pltpu.SemaphoreType.DMA
    work = 2 * fine_px * channels * span
    bank_bytes = 2 * banks * rows * span

    other_fb, other_cb = send(lambda x, d: over_batch(x, 1), (fb, cb), range(2))

    def mix_scratch():
        return [pltpu.SMEM(fc.shape, F32), pltpu.VMEM((2, banks, rows, span), BF16), pltpu.VMEM((pairs, block, span), BF16)]

    packs = call(
        functools.partial(pack_body, pairs),
        [shape(2 * coarse_px, block)] * pairs, hbm(2), hbm(pairs),
        [
            pltpu.VMEM((coarse_px, channels), BF16), pltpu.VMEM((coarse_px, width), BF16),
            dma((2,)), dma((2, pairs)),
        ],
        nbytes=bank_bytes, alone=True,
    )(cx, cup)
    bufs = to_pairs(packs)
    chunk = chunk_of(rows, count)
    fine_sum, fine_row, coarse_sum, coarse_row = call(
        functools.partial(tables_body, pairs, chunk),
        [shape(2 * banks * chunk, count * chunk), shape(1, 128, dtype=F32)] * 2,
        smem(2), vmem(4), flops=work, nbytes=bank_bytes,
    )(fc, cc)

    mixed = call(
        functools.partial(mix_body, pairs),
        [shape(block, span)] * pairs, hbm(3), hbm(pairs),
        mix_scratch() + [dma, dma((2, taps)), dma((pairs, taps))],
        flops=4 * banks * pairs * block * span, nbytes=3 * bank_bytes,
    )(fc, fb, other_fb)
    mixed = to_pairs(mixed)

    parts = call(
        functools.partial(coarse_body, pairs, coarse_side),
        [shape(coarse_px, block)] * pairs, hbm(3 + pairs), hbm(pairs),
        mix_scratch() + [
            pltpu.VMEM((pairs, coarse_px, width), BF16),
            pltpu.VMEM((coarse_px + 2 * coarse_side, 3 * width), BF16),
            pltpu.VMEM((pairs, coarse_px, block), BF16),
            dma, dma((2, taps)), dma((pairs,)), dma((pairs,)),
        ],
        flops=work, nbytes=3 * bank_bytes,
    )(cc, cb, other_cb, *bufs)

    front = call(
        functools.partial(front_body, pairs, fine_side),
        [shape(block, span)] * pairs, hbm(2), hbm(pairs),
        [
            pltpu.VMEM((fine_px, channels), BF16), pltpu.VMEM((fine_px, width), BF16),
            pltpu.VMEM((fine_px + 2 * fine_side, 3 * width), BF16), pltpu.VMEM((channels, span), BF16),
            dma((2,)), dma((pairs,)),
        ],
        flops=work, nbytes=5 * fine_px * channels,
    )(fx, fup)
    fine_own = to_pairs(front)

    fine_parts = call(
        functools.partial(delta_body, pairs, fine_side),
        [shape(fine_px, block)] * pairs, hbm(1 + pairs), hbm(pairs),
        [
            pltpu.VMEM((fine_px, width), BF16),
            pltpu.VMEM((fine_px + 2 * fine_side, 3 * width), BF16),
            pltpu.VMEM((channels, span), BF16), pltpu.VMEM((pairs, fine_px, block), BF16),
            dma((pairs + 1,)), dma((pairs,)),
        ],
        flops=work, nbytes=5 * fine_px * channels,
    )(fup, *mixed)
    fine_parts = [fine_parts[0]] + send(over_chan, fine_parts[1:], range(1, pairs))

    tile = shape(8, 128, dtype=F32)
    loaded = [shape(coarse_px + 16, block)]
    calm = call(
        functools.partial(calm_body, pairs, coarse_side),
        [shape(block, span)] * pairs + [shape(pairs, 128, dtype=F32)],
        hbm(2 + pairs), hbm(pairs) + vmem(1),
        [
            pltpu.VMEM((2, banks, rows, span), BF16), pltpu.VMEM((pairs, 2 * coarse_px, block), BF16),
            pltpu.VMEM((coarse_px + 2 * coarse_side, 3 * width), BF16),
            pltpu.VMEM((pairs, block, span), BF16),
            dma((2, taps)), dma((pairs,)), dma((pairs,)),
        ],
        flops=work, nbytes=3 * bank_bytes,
    )(cb, other_cb, *bufs)
    coarse_own, coarse_dcoef = calm[:pairs], calm[pairs]

    late = call(
        functools.partial(late_body, pairs),
        loaded * (pairs - 1) + [tile],
        hbm(2) + vmem(1) + hbm(2 * pairs - 1), hbm(pairs - 1) + vmem(1),
        [
            pltpu.VMEM((2, banks, rows, span), BF16), pltpu.VMEM((pairs, block, span), BF16),
            pltpu.VMEM((pairs - 1, coarse_px + 16, block), BF16),
            dma((2, taps)), dma((pairs,)), dma((pairs - 1,)), dma((pairs - 1,)),
        ],
        flops=work, nbytes=3 * bank_bytes,
    )(fb, other_fb, coarse_dcoef, *fine_own, *parts[1:])
    tiles = send(lambda x, d: over_batch(x, 2 * d), late[: pairs - 1], range(1, pairs))

    slots = call(
        functools.partial(slot_body, pairs),
        loaded * pairs + [tile],
        hbm(1) + vmem(1) + hbm(pairs - 1), hbm(pairs) + vmem(1),
        [pltpu.VMEM((pairs, coarse_px + 16, block), BF16), dma((pairs,)), dma((pairs,))],
        nbytes=4 * pairs * coarse_px * block,
    )(parts[0], late[pairs - 1], *tiles)
    slots, mine = slots[:pairs], slots[pairs]
    slots = [slots[0]] + send(over_chan, slots[1:], range(1, pairs))

    swapped = [
        send(lambda x, d: over_batch(x, 1), own, range(pairs))
        for own in (fine_own, coarse_own)
    ]

    def update(table, own, others):
        return call(
            functools.partial(update_body, pairs, 1),
            [shape(banks, taps, rows, width, dtype=F32)], vmem(1) + hbm(2 * pairs), hbm(1),
            [
                pltpu.VMEM((1, count, rows, span), BF16),
                pltpu.VMEM((1, banks, taps, rows, width), F32),
                dma((1, count)), dma((1, taps)),
            ],
            flops=2 * banks * count * rows * span, nbytes=3 * bank_bytes,
        )(table, *own, *others)[0]

    fine_update = update(fine_sum, fine_own, swapped[0])
    coarse_update = update(coarse_sum, coarse_own, swapped[1])

    fine_logit, coarse_logit, fine_delta, coarse_delta = call(
        functools.partial(final_body, pairs, banks),
        [shape(1, banks, dtype=F32)] * 2 + [shape(fine_px, block), shape(coarse_px, block)],
        vmem(3) + hbm(2 * pairs), vmem(2) + hbm(2),
        [
            pltpu.VMEM((pairs + 1, fine_px, block), BF16),
            pltpu.VMEM((pairs + 1, coarse_px + 16, block), BF16), dma((2, pairs)), dma((2,)),
        ],
        nbytes=2 * fine_px * channels,
    )(mine, fine_row, coarse_row, *fine_parts, *slots)
    fine_delta = fine_delta.reshape(1, fine_side, fine_side, block)
    coarse_delta = coarse_delta.reshape(1, coarse_side, coarse_side, block)
    return (fine_delta, fine_update, fine_logit, coarse_delta, coarse_update, coarse_logit)


def fits_pairs(mesh, fi, fu, fb, fc, ci, cu, cb, cc):
    count, pairs = mesh.shape["batch"], mesh.shape["chan"]
    rows, width, block = fb.shape[2] // count, fb.shape[3] // pairs, fb.shape[2] // pairs
    banks = fb.shape[0]
    return (
        count == 2 * pairs
        and pairs & (pairs - 1) == 0
        and fi.shape[0] == count
        and fb.shape == cb.shape
        and fi.shape[3] == fb.shape[2]
        and rows % 16 == 0
        and width % 128 == 0
        and block == width
        and all(x.shape[1] ** 2 % block == 0 for x in (fi, ci))
        and 2 * banks <= 128
        and all(x.shape[1] == x.shape[2] and x.shape[1] % 16 == 0 for x in (fi, ci))
    )


def solution(mesh):
    def step(*args):
        body = pair_device if fits_pairs(mesh, *args) else plain_device
        mapped = jax.shard_map(
            body,
            mesh=mesh,
            in_specs=(
                P("batch", None, None, None),
                P("batch", None, None, "chan"),
                P(None, None, "batch", "chan"),
                P(),
                P("batch", None, None, None),
                P("batch", None, None, "chan"),
                P(None, None, "batch", "chan"),
                P(),
            ),
            out_specs=(
                P("batch", None, None, "chan"),
                P(None, None, "batch", "chan"),
                P("batch", None),
                P("batch", None, None, "chan"),
                P(None, None, "batch", "chan"),
                P("batch", None),
            ),
            check_vma=False,
        )
        return mapped(*args)

    return step
```

profile of v0, /device:TPU:0, one launch (start us, length us, event | category | flops | bytes accessed | tf_op | source)
XLA Modules:
  0.0 95.9 jit_solution(17088002683872566731)
XLA Ops:
  0.6 0.6 collective-permute-start.4
  1.2 0.1 collective-permute-start
  1.3 1.8 %shard_map.127 = (bf16[512,128]{1,0:T(8,128)(2,1)}, bf16[512,128]{1,0:T(8,128)(2,1)}, bf16[512,128]{1,0:T(8,128)(2,1)}, bf16[512,128]{1,0:T(8,128)(2,1)}) custom-call(bf16[256,512]{1,0:T(8,128)(2,1)} %bitcast.9, bf16[256,128]{1,0:T(8,128)(2,1)} %bitcast.10), custom_call_target="tpu_custom_call" | custom-call | bytes 1179648 | tf_op jit(solution)/shard_map/pallas_call | solution.py:548
  3.0 3.0 %collective-permute-start.1 = (bf16[512,128]{1,0:T(8,128)(2,1)}, bf16[512,128]{1,0:T(8,128)(2,1)S(1)}, u32[]{:S(2)}, u32[]{:S(2)}) collective-permute-start(bf16[512,128]{1,0:T(8,128)(2,1)} %get-tuple-element.49), channel_id=1, source_target_pairs={{0,8},{4,12},{8,0},{12,4},{16,24},{20,28},{24,16},{28,20},{1,9},{5... | collective-permute-start | bytes 393224 | tf_op jit(solution)/shard_map/ppermute | solution.py:524
  6.0 1.5 %collective-permute-start.2 = (bf16[512,128]{1,0:T(8,128)(2,1)}, bf16[512,128]{1,0:T(8,128)(2,1)S(1)}, u32[]{:S(2)}, u32[]{:S(2)}) collective-permute-start(bf16[512,128]{1,0:T(8,128)(2,1)} %get-tuple-element.50), channel_id=1, source_target_pairs={{0,16},{4,20},{8,24},{12,28},{16,0},{20,4},{24,8},{28,12},{1,17},{... | collective-permute-start | bytes 393224 | tf_op jit(solution)/shard_map/ppermute | solution.py:524
  7.5 0.0 collective-permute-start.3
  7.5 1.2 %copy-done.3 = bf16[1,32,32,512]{3,2,1,0:T(8,128)(2,1)S(1)} copy-done((bf16[1,32,32,512]{3,2,1,0:T(8,128)(2,1)S(1)}, bf16[1,32,32,512]{3,2,1,0:T(8,128)(2,1)}, u32[]{:S(2)}) %copy-start.3) | copy-done | bytes 1048600
  8.8 0.9 copy-done.4
  9.7 2.1 %shard_map.130 = (bf16[128,1152]{1,0:T(8,128)(2,1)S(1)}, bf16[128,1152]{1,0:T(8,128)(2,1)S(1)}, bf16[128,1152]{1,0:T(8,128)(2,1)S(1)}, bf16[128,1152]{1,0:T(8,128)(2,1)S(1)}) custom-call(bf16[1024,512]{1,0:T(8,128)(2,1)S(1)} %bitcast.6, bf16[1024,128]{1,0:T(8,128)(2,1)S(1)} %bitcast.7), custom_call_target="tpu_custom_call" | custom-call | flops 1207959552 | bytes 2621440 | tf_op jit(solution)/shard_map/pallas_call | solution.py:585
  11.9 2.0 %collective-permute-start.5 = (bf16[128,1152]{1,0:T(8,128)(2,1)S(1)}, bf16[128,1152]{1,0:T(8,128)(2,1)S(1)}, u32[]{:S(2)}, u32[]{:S(2)}) collective-permute-start(bf16[128,1152]{1,0:T(8,128)(2,1)S(1)} %get-tuple-element.55), channel_id=1, source_target_pairs={{0,8},{4,12},{8,0},{12,4},{16,24},{20,28},{24,16},{28,20},{1,9},{5... | collective-permute-start | bytes 884744 | tf_op jit(solution)/shard_map/ppermute | solution.py:524
  13.9 0.3 collective-permute-done.2.rest_2_
  14.2 1.5 %collective-permute-start.6 = (bf16[128,1152]{1,0:T(8,128)(2,1)S(1)}, bf16[128,1152]{1,0:T(8,128)(2,1)S(1)}, u32[]{:S(2)}, u32[]{:S(2)}) collective-permute-start(bf16[128,1152]{1,0:T(8,128)(2,1)S(1)} %get-tuple-element.56), channel_id=1, source_target_pairs={{0,16},{4,20},{8,24},{12,28},{16,0},{20,4},{24,8},{28,12},{1,17},{... | collective-permute-start | bytes 884744 | tf_op jit(solution)/shard_map/ppermute | solution.py:524
  15.7 0.0 collective-permute-done.3.rest_3_
  15.7 0.0 collective-permute-start.7
  15.8 0.0 copy-start.2
  15.8 0.0 copy-start.6
  15.8 0.1 collective-permute-start.20
  15.9 2.6 %shard_map.134 = (bf16[128,1152]{1,0:T(8,128)(2,1)S(1)}, bf16[128,1152]{1,0:T(8,128)(2,1)S(1)}, bf16[128,1152]{1,0:T(8,128)(2,1)S(1)}, bf16[128,1152]{1,0:T(8,128)(2,1)S(1)}) custom-call(f32[8,8]{1,0:T(8,128)S(1)} %copy-done.1, bf16[8,9,64,128]{3,2,1,0:T(8,128)(2,1)S(1)} %copy-done, bf16[8,9,64,128]{3,2,1,0:T(8,128)(2,1)S(1)} %collective-permute-done.4.other), custom_call_target="tpu_custom_call" | custom-call | flops 18874368 | bytes 3538944 | tf_op jit(solution)/shard_map/pallas_call | solution.py:565
  18.5 3.3 %collective-permute-done.5.rest_1_.rest_2_ = bf16[128,1152]{1,0:T(8,128)(2,1)S(1)} collective-permute-done((bf16[128,1152]{1,0:T(8,128)(2,1)S(1)}, bf16[128,1152]{1,0:T(8,128)(2,1)S(1)}, u32[]{:S(2)}, u32[]{:S(2)}) %collective-permute-start.5) | collective-permute-done | bytes 294944 | tf_op jit(solution)/shard_map/ppermute | solution.py:524
  21.8 6.4 %collective-permute-done.6.rest_2_.rest_3_ = bf16[128,1152]{1,0:T(8,128)(2,1)S(1)} collective-permute-done((bf16[128,1152]{1,0:T(8,128)(2,1)S(1)}, bf16[128,1152]{1,0:T(8,128)(2,1)S(1)}, u32[]{:S(2)}, u32[]{:S(2)}) %collective-permute-start.6) | collective-permute-done | bytes 294944 | tf_op jit(solution)/shard_map/ppermute | solution.py:524
  28.2 0.5 collective-permute-start.23
  28.7 0.6 collective-permute-start.11
  29.4 3.7 %shard_map.129 = (bf16[128,1152]{1,0:T(8,128)(2,1)S(1)}, bf16[128,1152]{1,0:T(8,128)(2,1)S(1)}, bf16[128,1152]{1,0:T(8,128)(2,1)S(1)}, bf16[128,1152]{1,0:T(8,128)(2,1)S(1)}, f32[4,128]{1,0:T(4,128)S(1)}) custom-call(bf16[8,9,64,128]{3,2,1,0:T(8,128)(2,1)S(1)} %copy-done.2, bf16[8,9,64,128]{3,2,1,0:T(8,128)(2,1)S(1)} %collective-permute-done.other, ...), custom_call_target="tpu_custom_call" | custom-call | flops 1207959552 | bytes 3538944 | tf_op jit(solution)/shard_map/pallas_call | solution.py:612
  33.1 4.0 %shard_map.128 = (bf16[256,128]{1,0:T(8,128)(2,1)S(1)}, bf16[256,128]{1,0:T(8,128)(2,1)S(1)}, bf16[256,128]{1,0:T(8,128)(2,1)S(1)}, bf16[256,128]{1,0:T(8,128)(2,1)S(1)}) custom-call(f32[8,8]{1,0:T(8,128)S(1)} %copy-done.7, bf16[8,9,64,128]{3,2,1,0:T(8,128)(2,1)S(1)} %copy-done.2, bf16[8,9,64,128]{3,2,1,0:T(8,128)(2,1)S(1)} %collective-permute-done.other, ...), custom_call_target="tpu_custom_call" | custom-call | flops 1207959552 | bytes 3538944 | tf_op jit(solution)/shard_map/pallas_call | solution.py:573
  37.2 1.4 %collective-permute-start.12 = (bf16[128,1152]{1,0:T(8,128)(2,1)S(1)}, bf16[128,1152]{1,0:T(8,128)(2,1)S(1)}, u32[]{:S(2)}, u32[]{:S(2)}) collective-permute-start(bf16[128,1152]{1,0:T(8,128)(2,1)S(1)} %get-tuple-element.70), channel_id=1, source_target_pairs={{0,16},{4,20},{8,24},{12,28},{16,0},{20,4},{24,8},{28,12},{1,17},{... | collective-permute-start | bytes 884744 | tf_op jit(solution)/shard_map/ppermute | solution.py:524
  38.6 2.4 %shard_map.131 = (bf16[272,128]{1,0:T(8,128)(2,1)S(1)}, bf16[272,128]{1,0:T(8,128)(2,1)S(1)}, bf16[272,128]{1,0:T(8,128)(2,1)S(1)}, f32[8,128]{1,0:T(8,128)S(1)}) custom-call(bf16[8,9,64,128]{3,2,1,0:T(8,128)(2,1)S(1)} %copy-done, bf16[8,9,64,128]{3,2,1,0:T(8,128)(2,1)S(1)} %collective-permute-done.4.other, f32[4,128]{1,0:T(4,128)S(1)} %get-tuple-element.53.more, ...), custom_call_target="tpu_custom_call" | custom-call | flops 1207959552 | bytes 3538944 | tf_op jit(solution)/shard_map/pallas_call | solution.py:626
  41.0 1.6 %collective-permute-start.10 = (bf16[272,128]{1,0:T(8,128)(2,1)S(1)}, bf16[272,128]{1,0:T(8,128)(2,1)S(1)}, u32[]{:S(2)}, u32[]{:S(2)}) collective-permute-start(bf16[272,128]{1,0:T(8,128)(2,1)S(1)} %get-tuple-element.64), channel_id=1, source_target_pairs={{0,24},{4,28},{8,16},{12,20},{16,8},{20,12},{24,0},{28,4},{1,25},{... | collective-permute-start | bytes 208904 | tf_op jit(solution)/shard_map/ppermute | solution.py:524
  42.6 1.4 %collective-permute-start.13 = (bf16[128,1152]{1,0:T(8,128)(2,1)S(1)}, bf16[128,1152]{1,0:T(8,128)(2,1)S(1)}, u32[]{:S(2)}, u32[]{:S(2)}) collective-permute-start(bf16[128,1152]{1,0:T(8,128)(2,1)S(1)} %get-tuple-element.71), channel_id=1, source_target_pairs={{0,24},{4,28},{8,16},{12,20},{16,8},{20,12},{24,0},{28,4},{1,25},{... | collective-permute-start | bytes 884744 | tf_op jit(solution)/shard_map/ppermute | solution.py:524
  44.0 1.8 %collective-permute-start.8 = (bf16[272,128]{1,0:T(8,128)(2,1)S(1)}, bf16[272,128]{1,0:T(8,128)(2,1)S(1)}, u32[]{:S(2)}, u32[]{:S(2)}) collective-permute-start(bf16[272,128]{1,0:T(8,128)(2,1)S(1)} %get-tuple-element.62), channel_id=1, source_target_pairs={{0,8},{4,12},{8,0},{12,4},{16,24},{20,28},{24,16},{28,20},{1,9},{5... | collective-permute-start | bytes 208904 | tf_op jit(solution)/shard_map/ppermute | solution.py:524
  45.8 1.2 %collective-permute-done.10.rest_2_ = bf16[272,128]{1,0:T(8,128)(2,1)S(1)} collective-permute-done((bf16[272,128]{1,0:T(8,128)(2,1)S(1)}, bf16[272,128]{1,0:T(8,128)(2,1)S(1)}, u32[]{:S(2)}, u32[]{:S(2)}) %collective-permute-start.10) | collective-permute-done | bytes 69664 | tf_op jit(solution)/shard_map/ppermute | solution.py:524
  47.0 6.4 %collective-permute-done.8.rest_0_ = bf16[272,128]{1,0:T(8,128)(2,1)S(1)} collective-permute-done((bf16[272,128]{1,0:T(8,128)(2,1)S(1)}, bf16[272,128]{1,0:T(8,128)(2,1)S(1)}, u32[]{:S(2)}, u32[]{:S(2)}) %collective-permute-start.8) | collective-permute-done | bytes 69664 | tf_op jit(solution)/shard_map/ppermute | solution.py:524
  53.4 2.3 %collective-permute-done.9.rest_1_ = bf16[272,128]{1,0:T(8,128)(2,1)S(1)} collective-permute-done((bf16[272,128]{1,0:T(8,128)(2,1)S(1)}, bf16[272,128]{1,0:T(8,128)(2,1)S(1)}, u32[]{:S(2)}, u32[]{:S(2)}) %collective-permute-start.9) | collective-permute-done | bytes 69664 | tf_op jit(solution)/shard_map/ppermute | solution.py:524
  55.7 0.5 collective-permute-start.26
  56.2 0.1 collective-permute-start.27
  56.3 0.8 shard_map.132
  57.1 1.6 %collective-permute-start.17 = (bf16[272,128]{1,0:T(8,128)(2,1)S(1)}, bf16[272,128]{1,0:T(8,128)(2,1)S(1)}, u32[]{:S(2)}, u32[]{:S(2)}) collective-permute-start(bf16[272,128]{1,0:T(8,128)(2,1)S(1)} %get-tuple-element.77), channel_id=1, source_target_pairs={{0,1},{1,0},{2,3},{3,2},{4,5},{5,4},{6,7},{7,6},{8,9},{9,8},{10,11... | collective-permute-start | bytes 208904 | tf_op jit(solution)/shard_map/ppermute | solution.py:527
  58.7 2.4 %shard_map.135 = (bf16[1024,128]{1,0:T(8,128)(2,1)S(1)}, bf16[1024,128]{1,0:T(8,128)(2,1)S(1)}, bf16[1024,128]{1,0:T(8,128)(2,1)S(1)}, bf16[1024,128]{1,0:T(8,128)(2,1)S(1)}) custom-call(bf16[1024,128]{1,0:T(8,128)(2,1)S(1)} %bitcast.8, bf16[128,1152]{1,0:T(8,128)(2,1)S(1)} %get-tuple-element.68.rest_0_, ...), custom_call_target="tpu_custom_call" | custom-call | flops 1207959552 | bytes 2621440 | tf_op jit(solution)/shard_map/pallas_call | solution.py:597
  61.1 0.5 collective-permute-done.17.rest_5_
  61.6 1.6 %collective-permute-start.14 = (bf16[1024,128]{1,0:T(8,128)(2,1)S(1)}, bf16[1024,128]{1,0:T(8,128)(2,1)S(1)}, u32[]{:S(2)}, u32[]{:S(2)}) collective-permute-start(bf16[1024,128]{1,0:T(8,128)(2,1)S(1)} %get-tuple-element.73), channel_id=1, source_target_pairs={{0,1},{1,0},{2,3},{3,2},{4,5},{5,4},{6,7},{7,6},{8,9},{9,8},{10,11... | collective-permute-start | bytes 786440 | tf_op jit(solution)/shard_map/ppermute | solution.py:527
  63.2 2.6 %collective-permute-start.15 = (bf16[1024,128]{1,0:T(8,128)(2,1)S(1)}, bf16[1024,128]{1,0:T(8,128)(2,1)S(1)}, u32[]{:S(2)}, u32[]{:S(2)}) collective-permute-start(bf16[1024,128]{1,0:T(8,128)(2,1)S(1)} %get-tuple-element.74), channel_id=1, source_target_pairs={{0,2},{1,3},{2,0},{3,1},{4,6},{5,7},{6,4},{7,5},{8,10},{9,11},{10,... | collective-permute-start | bytes 786440 | tf_op jit(solution)/shard_map/ppermute | solution.py:527
  65.8 0.2 collective-permute-start.16
  66.0 1.7 %collective-permute-start.18 = (bf16[272,128]{1,0:T(8,128)(2,1)S(1)}, bf16[272,128]{1,0:T(8,128)(2,1)S(1)}, u32[]{:S(2)}, u32[]{:S(2)}) collective-permute-start(bf16[272,128]{1,0:T(8,128)(2,1)S(1)} %get-tuple-element.78), channel_id=1, source_target_pairs={{0,2},{1,3},{2,0},{3,1},{4,6},{5,7},{6,4},{7,5},{8,10},{9,11},{10,... | collective-permute-start | bytes 208904 | tf_op jit(solution)/shard_map/ppermute | solution.py:527
  67.7 2.0 %collective-permute-start.19 = (bf16[272,128]{1,0:T(8,128)(2,1)S(1)}, bf16[272,128]{1,0:T(8,128)(2,1)S(1)}, u32[]{:S(2)}, u32[]{:S(2)}) collective-permute-start(bf16[272,128]{1,0:T(8,128)(2,1)S(1)} %get-tuple-element.79), channel_id=1, source_target_pairs={{0,3},{1,2},{2,1},{3,0},{4,7},{5,6},{6,5},{7,4},{8,11},{9,10},{10,... | collective-permute-start | bytes 208904 | tf_op jit(solution)/shard_map/ppermute | solution.py:527
  69.7 0.8 shard_map.133
  70.5 3.7 %shard_map.137 = f32[8,9,64,128]{3,2,1,0:T(8,128)} custom-call(bf16[512,256]{1,0:T(8,128)(2,1)S(1)} %get-tuple-element.81.rest_0_, bf16[128,1152]{1,0:T(8,128)(2,1)S(1)} %get-tuple-element.54.rest_0_.rest_1_, bf16[128,1152]{1,0:T(8,128)(2,1)S(1)} %collective-permute-done.5.rest_1_.rest_2_, bf16[128,1152]{1,0:T(8,128)(2,1)S(1)} %collective-permute-done.6.rest_2_.rest_3_, ...), custom_call_target="tpu_custom_call" | custom-call | flops 9437184 | bytes 3538944 | tf_op jit(solution)/shard_map/pallas_call | solution.py:655
  74.2 3.7 %shard_map.138 = f32[8,9,64,128]{3,2,1,0:T(8,128)} custom-call(bf16[512,256]{1,0:T(8,128)(2,1)S(1)} %get-tuple-element.84.rest_0_, bf16[128,1152]{1,0:T(8,128)(2,1)S(1)} %get-tuple-element.85.rest_1_, bf16[128,1152]{1,0:T(8,128)(2,1)S(1)} %get-tuple-element.86.rest_2_, bf16[128,1152]{1,0:T(8,128)(2,1)S(1)} %get-tuple-element.87.rest_3_, ...), custom_call_target="tpu_custom_call" | custom-call | flops 9437184 | bytes 3538944 | tf_op jit(solution)/shard_map/pallas_call | solution.py:655
  77.9 15.9 %collective-permute-done.18.rest_6_ = bf16[272,128]{1,0:T(8,128)(2,1)S(1)} collective-permute-done((bf16[272,128]{1,0:T(8,128)(2,1)S(1)}, bf16[272,128]{1,0:T(8,128)(2,1)S(1)}, u32[]{:S(2)}, u32[]{:S(2)}) %collective-permute-start.18) | collective-permute-done | bytes 69664 | tf_op jit(solution)/shard_map/ppermute | solution.py:527
  93.8 2.0 %shard_map.136 = (f32[1,8]{1,0:T(1,128)}, f32[1,8]{1,0:T(1,128)}, bf16[1024,128]{1,0:T(8,128)(2,1)}, bf16[256,128]{1,0:T(8,128)(2,1)}) custom-call(f32[8,128]{1,0:T(8,128)S(1)} %get-tuple-element.65.mine, f32[1,128]{1,0:T(1,128)S(1)} %get-tuple-element.66.fine_row, f32[1,128]{1,0:T(1,128)S(1)} %get-tuple-element.67.coarse_row, ...), custom_call_target="tpu_custom_call" | custom-call | bytes 1048576 | tf_op jit(solution)/shard_map/pallas_call | solution.py:669
  (36 shorter events, 0.1 us)
Async XLA Ops:
  0.6 15.1 %collective-permute-start.4 = (bf16[8,9,64,128]{3,2,1,0:T(8,128)(2,1)}, bf16[8,9,64,128]{3,2,1,0:T(8,128)(2,1)S(1)}, u32[]{:S(2)}, u32[]{:S(2)}) collective-permute-start(bf16[8,9,64,128]{3,2,1,0:T(8,128)(2,1)} %own.7), channel_id=1, source_target_pairs={{0,4},{4,0},{8,12},{12,8},{16,20},{20,16},{24,28},{28,24},{1,5},{5... | collective-permute-start | bytes 3538952 | tf_op jit(solution)/shard_map/ppermute | solution.py:524
  1.2 27.5 %collective-permute-start = (bf16[8,9,64,128]{3,2,1,0:T(8,128)(2,1)}, bf16[8,9,64,128]{3,2,1,0:T(8,128)(2,1)S(1)}, u32[]{:S(2)}, u32[]{:S(2)}) collective-permute-start(bf16[8,9,64,128]{3,2,1,0:T(8,128)(2,1)} %own.5), channel_id=1, source_target_pairs={{0,4},{4,0},{8,12},{12,8},{16,20},{20,16},{24,28},{28,24},{1,5},{5... | collective-permute-start | bytes 3538952 | tf_op jit(solution)/shard_map/ppermute | solution.py:524
  3.0 8.9 %collective-permute-start.1 = (bf16[512,128]{1,0:T(8,128)(2,1)}, bf16[512,128]{1,0:T(8,128)(2,1)S(1)}, u32[]{:S(2)}, u32[]{:S(2)}) collective-permute-start(bf16[512,128]{1,0:T(8,128)(2,1)} %get-tuple-element.49), channel_id=1, source_target_pairs={{0,8},{4,12},{8,0},{12,4},{16,24},{20,28},{24,16},{28,20},{1,9},{5... | collective-permute-start | bytes 393224 | tf_op jit(solution)/shard_map/ppermute | solution.py:524
  6.0 8.2 %collective-permute-start.2 = (bf16[512,128]{1,0:T(8,128)(2,1)}, bf16[512,128]{1,0:T(8,128)(2,1)S(1)}, u32[]{:S(2)}, u32[]{:S(2)}) collective-permute-start(bf16[512,128]{1,0:T(8,128)(2,1)} %get-tuple-element.50), channel_id=1, source_target_pairs={{0,16},{4,20},{8,24},{12,28},{16,0},{20,4},{24,8},{28,12},{1,17},{... | collective-permute-start | bytes 393224 | tf_op jit(solution)/shard_map/ppermute | solution.py:524
  7.5 8.2 %collective-permute-start.3 = (bf16[512,128]{1,0:T(8,128)(2,1)}, bf16[512,128]{1,0:T(8,128)(2,1)S(1)}, u32[]{:S(2)}, u32[]{:S(2)}) collective-permute-start(bf16[512,128]{1,0:T(8,128)(2,1)} %get-tuple-element.51), channel_id=1, source_target_pairs={{0,24},{4,28},{8,16},{12,20},{16,8},{20,12},{24,0},{28,4},{1,25},{... | collective-permute-start | bytes 393224 | tf_op jit(solution)/shard_map/ppermute | solution.py:524
  7.5 1.2 %copy-start.3 = (bf16[1,32,32,512]{3,2,1,0:T(8,128)(2,1)S(1)}, bf16[1,32,32,512]{3,2,1,0:T(8,128)(2,1)}, u32[]{:S(2)}) copy-start(bf16[1,32,32,512]{3,2,1,0:T(8,128)(2,1)} %param.8) | copy-start | bytes 3145732
  8.8 0.9 copy-start.4
  9.7 6.1 %copy-start = (bf16[8,9,64,128]{3,2,1,0:T(8,128)(2,1)S(1)}, bf16[8,9,64,128]{3,2,1,0:T(8,128)(2,1)}, u32[]{:S(2)}) copy-start(bf16[8,9,64,128]{3,2,1,0:T(8,128)(2,1)} %own.7) | copy-start | bytes 3538948
  9.7 6.2 %copy-start.1 = (f32[8,8]{1,0:T(8,128)S(1)}, f32[8,8]{1,0:T(8,128)}, u32[]{:S(2)}) copy-start(f32[8,8]{1,0:T(8,128)} %coefs.3) | copy-start | bytes 772
  11.9 9.9 %collective-permute-start.5 = (bf16[128,1152]{1,0:T(8,128)(2,1)S(1)}, bf16[128,1152]{1,0:T(8,128)(2,1)S(1)}, u32[]{:S(2)}, u32[]{:S(2)}) collective-permute-start(bf16[128,1152]{1,0:T(8,128)(2,1)S(1)} %get-tuple-element.55), channel_id=1, source_target_pairs={{0,8},{4,12},{8,0},{12,4},{16,24},{20,28},{24,16},{28,20},{1,9},{5... | collective-permute-start | bytes 884744 | tf_op jit(solution)/shard_map/ppermute | solution.py:524
  14.2 14.0 %collective-permute-start.6 = (bf16[128,1152]{1,0:T(8,128)(2,1)S(1)}, bf16[128,1152]{1,0:T(8,128)(2,1)S(1)}, u32[]{:S(2)}, u32[]{:S(2)}) collective-permute-start(bf16[128,1152]{1,0:T(8,128)(2,1)S(1)} %get-tuple-element.56), channel_id=1, source_target_pairs={{0,16},{4,20},{8,24},{12,28},{16,0},{20,4},{24,8},{28,12},{1,17},{... | collective-permute-start | bytes 884744 | tf_op jit(solution)/shard_map/ppermute | solution.py:524
  15.7 12.5 %collective-permute-start.7 = (bf16[128,1152]{1,0:T(8,128)(2,1)S(1)}, bf16[128,1152]{1,0:T(8,128)(2,1)S(1)}, u32[]{:S(2)}, u32[]{:S(2)}) collective-permute-start(bf16[128,1152]{1,0:T(8,128)(2,1)S(1)} %get-tuple-element.57), channel_id=1, source_target_pairs={{0,24},{4,28},{8,16},{12,20},{16,8},{20,12},{24,0},{28,4},{1,25},{... | collective-permute-start | bytes 884744 | tf_op jit(solution)/shard_map/ppermute | solution.py:524
  15.8 13.6 %copy-start.2 = (bf16[8,9,64,128]{3,2,1,0:T(8,128)(2,1)S(1)}, bf16[8,9,64,128]{3,2,1,0:T(8,128)(2,1)}, u32[]{:S(2)}) copy-start(bf16[8,9,64,128]{3,2,1,0:T(8,128)(2,1)} %own.5) | copy-start | bytes 3538948
  15.8 13.6 %copy-start.6 = (bf16[512,128]{1,0:T(8,128)(2,1)S(1)}, bf16[512,128]{1,0:T(8,128)(2,1)}, u32[]{:S(2)}) copy-start(bf16[512,128]{1,0:T(8,128)(2,1)} %get-tuple-element.48.rest_0_) | copy-start | bytes 393220
  15.8 21.4 %collective-permute-start.20 = (bf16[128,1152]{1,0:T(8,128)(2,1)S(1)}, bf16[128,1152]{1,0:T(8,128)(2,1)S(1)}, u32[]{:S(2)}, u32[]{:S(2)}) collective-permute-start(bf16[128,1152]{1,0:T(8,128)(2,1)S(1)} %get-tuple-element.54.rest_0_.rest_1_), channel_id=1, source_target_pairs={{0,4},{4,0},{8,12},{12,8},{16,20},{20,16},{24,28},{28,24},{1,5},{5... | collective-permute-start | bytes 884744 | tf_op jit(solution)/shard_map/ppermute | solution.py:524
  21.8 19.1 %collective-permute-start.21 = (bf16[128,1152]{1,0:T(8,128)(2,1)S(1)}, bf16[128,1152]{1,0:T(8,128)(2,1)S(1)}, u32[]{:S(2)}, u32[]{:S(2)}) collective-permute-start(bf16[128,1152]{1,0:T(8,128)(2,1)S(1)} %collective-permute-done.5.rest_1_.rest_2_), channel_id=1, source_target_pairs={{0,4},{4,0},{8,12},{12,8},{16,20},{20,16},{24,28},{28,24},{1,5},{5... | collective-permute-start | bytes 884744 | tf_op jit(solution)/shard_map/ppermute | solution.py:524
  28.2 14.4 %collective-permute-start.22 = (bf16[128,1152]{1,0:T(8,128)(2,1)S(1)}, bf16[128,1152]{1,0:T(8,128)(2,1)S(1)}, u32[]{:S(2)}, u32[]{:S(2)}) collective-permute-start(bf16[128,1152]{1,0:T(8,128)(2,1)S(1)} %collective-permute-done.6.rest_2_.rest_3_), channel_id=1, source_target_pairs={{0,4},{4,0},{8,12},{12,8},{16,20},{20,16},{24,28},{28,24},{1,5},{5... | collective-permute-start | bytes 884744 | tf_op jit(solution)/shard_map/ppermute | solution.py:524
  28.2 15.8 %collective-permute-start.23 = (bf16[128,1152]{1,0:T(8,128)(2,1)S(1)}, bf16[128,1152]{1,0:T(8,128)(2,1)S(1)}, u32[]{:S(2)}, u32[]{:S(2)}) collective-permute-start(bf16[128,1152]{1,0:T(8,128)(2,1)S(1)} %collective-permute-done.7.rest_3_.rest_4_), channel_id=1, source_target_pairs={{0,4},{4,0},{8,12},{12,8},{16,20},{20,16},{24,28},{28,24},{1,5},{5... | collective-permute-start | bytes 884744 | tf_op jit(solution)/shard_map/ppermute | solution.py:524
  28.7 27.0 %collective-permute-start.11 = (bf16[128,1152]{1,0:T(8,128)(2,1)S(1)}, bf16[128,1152]{1,0:T(8,128)(2,1)S(1)}, u32[]{:S(2)}, u32[]{:S(2)}) collective-permute-start(bf16[128,1152]{1,0:T(8,128)(2,1)S(1)} %get-tuple-element.69), channel_id=1, source_target_pairs={{0,8},{4,12},{8,0},{12,4},{16,24},{20,28},{24,16},{28,20},{1,9},{5... | collective-permute-start | bytes 884744 | tf_op jit(solution)/shard_map/ppermute | solution.py:524
  29.3 3.8 %copy-start.7 = (f32[8,8]{1,0:T(8,128)S(1)}, f32[8,8]{1,0:T(8,128)}, u32[]{:S(2)}) copy-start(f32[8,8]{1,0:T(8,128)} %coarse_coefs.1) | copy-start | bytes 772
  37.2 19.0 %collective-permute-start.12 = (bf16[128,1152]{1,0:T(8,128)(2,1)S(1)}, bf16[128,1152]{1,0:T(8,128)(2,1)S(1)}, u32[]{:S(2)}, u32[]{:S(2)}) collective-permute-start(bf16[128,1152]{1,0:T(8,128)(2,1)S(1)} %get-tuple-element.70), channel_id=1, source_target_pairs={{0,16},{4,20},{8,24},{12,28},{16,0},{20,4},{24,8},{28,12},{1,17},{... | collective-permute-start | bytes 884744 | tf_op jit(solution)/shard_map/ppermute | solution.py:524
  38.6 20.1 %copy-start.5 = (bf16[1,32,32,128]{3,2,1,0:T(8,128)(2,1)S(1)}, bf16[1,32,32,128]{3,2,1,0:T(8,128)(2,1)}, u32[]{:S(2)}) copy-start(bf16[1,32,32,128]{3,2,1,0:T(8,128)(2,1)} %param.9) | copy-start | bytes 786436
  41.0 6.0 %collective-permute-start.10 = (bf16[272,128]{1,0:T(8,128)(2,1)S(1)}, bf16[272,128]{1,0:T(8,128)(2,1)S(1)}, u32[]{:S(2)}, u32[]{:S(2)}) collective-permute-start(bf16[272,128]{1,0:T(8,128)(2,1)S(1)} %get-tuple-element.64), channel_id=1, source_target_pairs={{0,24},{4,28},{8,16},{12,20},{16,8},{20,12},{24,0},{28,4},{1,25},{... | collective-permute-start | bytes 208904 | tf_op jit(solution)/shard_map/ppermute | solution.py:524
  42.6 14.5 %collective-permute-start.13 = (bf16[128,1152]{1,0:T(8,128)(2,1)S(1)}, bf16[128,1152]{1,0:T(8,128)(2,1)S(1)}, u32[]{:S(2)}, u32[]{:S(2)}) collective-permute-start(bf16[128,1152]{1,0:T(8,128)(2,1)S(1)} %get-tuple-element.71), channel_id=1, source_target_pairs={{0,24},{4,28},{8,16},{12,20},{16,8},{20,12},{24,0},{28,4},{1,25},{... | collective-permute-start | bytes 884744 | tf_op jit(solution)/shard_map/ppermute | solution.py:524
  44.0 9.4 %collective-permute-start.8 = (bf16[272,128]{1,0:T(8,128)(2,1)S(1)}, bf16[272,128]{1,0:T(8,128)(2,1)S(1)}, u32[]{:S(2)}, u32[]{:S(2)}) collective-permute-start(bf16[272,128]{1,0:T(8,128)(2,1)S(1)} %get-tuple-element.62), channel_id=1, source_target_pairs={{0,8},{4,12},{8,0},{12,4},{16,24},{20,28},{24,16},{28,20},{1,9},{5... | collective-permute-start | bytes 208904 | tf_op jit(solution)/shard_map/ppermute | solution.py:524
  47.0 8.7 %collective-permute-start.9 = (bf16[272,128]{1,0:T(8,128)(2,1)S(1)}, bf16[272,128]{1,0:T(8,128)(2,1)S(1)}, u32[]{:S(2)}, u32[]{:S(2)}) collective-permute-start(bf16[272,128]{1,0:T(8,128)(2,1)S(1)} %get-tuple-element.63), channel_id=1, source_target_pairs={{0,16},{4,20},{8,24},{12,28},{16,0},{20,4},{24,8},{28,12},{1,17},{... | collective-permute-start | bytes 208904 | tf_op jit(solution)/shard_map/ppermute | solution.py:524
  53.4 9.9 %collective-permute-start.24 = (bf16[128,1152]{1,0:T(8,128)(2,1)S(1)}, bf16[128,1152]{1,0:T(8,128)(2,1)S(1)}, u32[]{:S(2)}, u32[]{:S(2)}) collective-permute-start(bf16[128,1152]{1,0:T(8,128)(2,1)S(1)} %get-tuple-element.85.rest_1_), channel_id=1, source_target_pairs={{0,4},{4,0},{8,12},{12,8},{16,20},{20,16},{24,28},{28,24},{1,5},{5... | collective-permute-start | bytes 884744 | tf_op jit(solution)/shard_map/ppermute | solution.py:524
  55.7 10.1 %collective-permute-start.25 = (bf16[128,1152]{1,0:T(8,128)(2,1)S(1)}, bf16[128,1152]{1,0:T(8,128)(2,1)S(1)}, u32[]{:S(2)}, u32[]{:S(2)}) collective-permute-start(bf16[128,1152]{1,0:T(8,128)(2,1)S(1)} %get-tuple-element.86.rest_2_), channel_id=1, source_target_pairs={{0,4},{4,0},{8,12},{12,8},{16,20},{20,16},{24,28},{28,24},{1,5},{5... | collective-permute-start | bytes 884744 | tf_op jit(solution)/shard_map/ppermute | solution.py:524
  55.7 10.4 %collective-permute-start.26 = (bf16[128,1152]{1,0:T(8,128)(2,1)S(1)}, bf16[128,1152]{1,0:T(8,128)(2,1)S(1)}, u32[]{:S(2)}, u32[]{:S(2)}) collective-permute-start(bf16[128,1152]{1,0:T(8,128)(2,1)S(1)} %get-tuple-element.87.rest_3_), channel_id=1, source_target_pairs={{0,4},{4,0},{8,12},{12,8},{16,20},{20,16},{24,28},{28,24},{1,5},{5... | collective-permute-start | bytes 884744 | tf_op jit(solution)/shard_map/ppermute | solution.py:524
  56.2 11.5 %collective-permute-start.27 = (bf16[128,1152]{1,0:T(8,128)(2,1)S(1)}, bf16[128,1152]{1,0:T(8,128)(2,1)S(1)}, u32[]{:S(2)}, u32[]{:S(2)}) collective-permute-start(bf16[128,1152]{1,0:T(8,128)(2,1)S(1)} %get-tuple-element.88.rest_4_), channel_id=1, source_target_pairs={{0,4},{4,0},{8,12},{12,8},{16,20},{20,16},{24,28},{28,24},{1,5},{5... | collective-permute-start | bytes 884744 | tf_op jit(solution)/shard_map/ppermute | solution.py:524
  57.1 4.6 %collective-permute-start.17 = (bf16[272,128]{1,0:T(8,128)(2,1)S(1)}, bf16[272,128]{1,0:T(8,128)(2,1)S(1)}, u32[]{:S(2)}, u32[]{:S(2)}) collective-permute-start(bf16[272,128]{1,0:T(8,128)(2,1)S(1)} %get-tuple-element.77), channel_id=1, source_target_pairs={{0,1},{1,0},{2,3},{3,2},{4,5},{5,4},{6,7},{7,6},{8,9},{9,8},{10,11... | collective-permute-start | bytes 208904 | tf_op jit(solution)/shard_map/ppermute | solution.py:527
  61.6 32.1 %collective-permute-start.14 = (bf16[1024,128]{1,0:T(8,128)(2,1)S(1)}, bf16[1024,128]{1,0:T(8,128)(2,1)S(1)}, u32[]{:S(2)}, u32[]{:S(2)}) collective-permute-start(bf16[1024,128]{1,0:T(8,128)(2,1)S(1)} %get-tuple-element.73), channel_id=1, source_target_pairs={{0,1},{1,0},{2,3},{3,2},{4,5},{5,4},{6,7},{7,6},{8,9},{9,8},{10,11... | collective-permute-start | bytes 786440 | tf_op jit(solution)/shard_map/ppermute | solution.py:527
  63.2 30.5 %collective-permute-start.15 = (bf16[1024,128]{1,0:T(8,128)(2,1)S(1)}, bf16[1024,128]{1,0:T(8,128)(2,1)S(1)}, u32[]{:S(2)}, u32[]{:S(2)}) collective-permute-start(bf16[1024,128]{1,0:T(8,128)(2,1)S(1)} %get-tuple-element.74), channel_id=1, source_target_pairs={{0,2},{1,3},{2,0},{3,1},{4,6},{5,7},{6,4},{7,5},{8,10},{9,11},{10,... | collective-permute-start | bytes 786440 | tf_op jit(solution)/shard_map/ppermute | solution.py:527
  65.8 28.0 %collective-permute-start.16 = (bf16[1024,128]{1,0:T(8,128)(2,1)S(1)}, bf16[1024,128]{1,0:T(8,128)(2,1)S(1)}, u32[]{:S(2)}, u32[]{:S(2)}) collective-permute-start(bf16[1024,128]{1,0:T(8,128)(2,1)S(1)} %get-tuple-element.75), channel_id=1, source_target_pairs={{0,3},{1,2},{2,1},{3,0},{4,7},{5,6},{6,5},{7,4},{8,11},{9,10},{10,... | collective-permute-start | bytes 786440 | tf_op jit(solution)/shard_map/ppermute | solution.py:527
  66.0 27.7 %collective-permute-start.18 = (bf16[272,128]{1,0:T(8,128)(2,1)S(1)}, bf16[272,128]{1,0:T(8,128)(2,1)S(1)}, u32[]{:S(2)}, u32[]{:S(2)}) collective-permute-start(bf16[272,128]{1,0:T(8,128)(2,1)S(1)} %get-tuple-element.78), channel_id=1, source_target_pairs={{0,2},{1,3},{2,0},{3,1},{4,6},{5,7},{6,4},{7,5},{8,10},{9,11},{10,... | collective-permute-start | bytes 208904 | tf_op jit(solution)/shard_map/ppermute | solution.py:527
  67.7 26.0 %collective-permute-start.19 = (bf16[272,128]{1,0:T(8,128)(2,1)S(1)}, bf16[272,128]{1,0:T(8,128)(2,1)S(1)}, u32[]{:S(2)}, u32[]{:S(2)}) collective-permute-start(bf16[272,128]{1,0:T(8,128)(2,1)S(1)} %get-tuple-element.79), channel_id=1, source_target_pairs={{0,3},{1,2},{2,1},{3,0},{4,7},{5,6},{6,5},{7,4},{8,11},{9,10},{10,... | collective-permute-start | bytes 208904 | tf_op jit(solution)/shard_map/ppermute | solution.py:527
where the time goes:
time: 96.2 us; the launch traced here: 95.9 us
  waiting for transfers between devices  36.3 us (38%)
  Pallas kernels  30 us (31%)
  starting transfers between devices  26.4 us (27%)
  local copies, waits for them, and re-layouts  2.2 us (2%)
  between operations  1 us (1%)
    ppermute x22, waiting for transfers between devices, over_batch(): return lax.ppermute(x, 'batch', [(i, i ^ d) for i in range(count)])  20 us
    ppermute x22, starting transfers between devices, over_batch(): return lax.ppermute(x, 'batch', [(i, i ^ d) for i in range(count)])  16.7 us
    ppermute x6, waiting for transfers between devices, over_chan(): return lax.ppermute(x, 'chan', [(i, i ^ d) for i in range(pairs)])  16.4 us
    ppermute x6, starting transfers between devices, over_chan(): return lax.ppermute(x, 'chan', [(i, i ^ d) for i in range(pairs)])  9.71 us
    pallas_call x2, Pallas kernels, update(): call(functools.partial(update_body, pairs, 1), [shape(banks, taps, rows,...  7.35 us
    pallas_call x1, Pallas kernels, pair_steps(): call(functools.partial(coarse_body, pairs, coarse_side), [shape(coarse_px...  4.04 us
    pallas_call x1, Pallas kernels, pair_steps(): call(functools.partial(calm_body, pairs, coarse_side), [shape(block, span...  3.74 us
    pallas_call x1, Pallas kernels, pair_steps(): call(functools.partial(mix_body, pairs), [shape(block, span)] * pairs, hb...  2.62 us
  transfers between devices with their start and end apart: 28, of which 8 were waited for; matrix products, arithmetic and copies ran while one was open for 0% of the time, Pallas kernels for 29%

commit v1 on v0

--- a/solution.py
+++ b/solution.py
@@ -91,14 +91,14 @@
     return [pl.BlockSpec(memory_space=pltpu.VMEM) for _ in range(n)]
 
 
-def call(body, out_shapes, in_specs, out_specs, scratch=(), flops=0, nbytes=0, alone=False, grant=16 * 1024 * 1024):
+def call(body, out_shapes, in_specs, out_specs, scratch=(), flops=0, nbytes=0, grant=16 * 1024 * 1024):
     return pl.pallas_call(
         body,
         out_shape=out_shapes,
         in_specs=in_specs,
         out_specs=out_specs,
         scratch_shapes=list(scratch),
-        compiler_params=pltpu.CompilerParams(vmem_limit_bytes=None if alone else grant),
+        compiler_params=pltpu.CompilerParams(vmem_limit_bytes=grant),
         cost_estimate=pl.CostEstimate(flops=flops, bytes_accessed=nbytes, transcendentals=0),
     )
 
@@ -260,11 +260,11 @@
     first.wait()
     table = spread(mix_weights(pairs, s_coefs), chunk_of(own.shape[2], own.shape[0]))
     stores = []
-    for t in range(0, taps, 3):
-        for some in loads[t : t + 3]:
+    for t in range(0, taps, 4):
+        for some in loads[t : t + 4]:
             for load in some:
                 load.wait()
-        lanes = slice(t * width, (t + 3) * width)
+        lanes = slice(t * width, min(t + 4, taps) * width)
         mix_lanes(pairs, table, v_banks, staged, lanes)
         for d, out in enumerate(outs):
             stores.append(start(staged.at[d, :, lanes], out.at[:, lanes], sem_out.at[d, t]))
@@ -330,11 +330,11 @@
     bank_loads = load_banks(own, other, v_banks, sem_bank)
     first.wait()
     table = spread(mix_weights(pairs, s_coefs), chunk_of(own.shape[2], own.shape[0]))
-    for t in range(0, taps, 3):
-        for some in bank_loads[t : t + 3]:
+    for t in range(0, taps, 4):
+        for some in bank_loads[t : t + 4]:
             for load in some:
                 load.wait()
-        mix_lanes(pairs, table, v_banks, v_mixed, slice(t * width, (t + 3) * width))
+        mix_lanes(pairs, table, v_banks, v_mixed, slice(t * width, min(t + 4, taps) * width))
     stores = []
     third = windows.shape[1]
     for d in range(pairs):
@@ -468,36 +468,37 @@
         store.wait()
 
 
+def sum_body(pairs, *rest):
+    pieces, (out, held, sem_in, sem_out) = rest[:pairs], rest[pairs:]
+    loads = [start(pieces[d], held.at[d], sem_in.at[d]) for d in range(pairs)]
+    for load in loads:
+        load.wait()
+    total = held[0].astype(F32)
+    for d in range(1, pairs):
+        total = total + held[d].astype(F32)
+    held[pairs] = total.astype(BF16)
+    start(held.at[pairs], out, sem_out).wait()
+
+
 def final_body(pairs, banks, mine, fine_row, coarse_row, *rest):
-    pieces, rest = rest[: 2 * pairs], rest[2 * pairs :]
-    fine_out, coarse_out, fine_delta, coarse_delta, v_fine, v_coarse, sem_in, sem_out = rest
-    layers = ((v_fine, fine_delta), (v_coarse, coarse_delta))
-    loads = [
-        [
-            start(pieces[n * pairs + d], v.at[d], sem_in.at[n, d])
-            for d in range(pairs)
-        ]
-        for n, (v, _) in enumerate(layers)
-    ]
-    stores = []
-    for n, (v, out) in enumerate(layers):
-        for load in loads[n]:
-            load.wait()
-        pixels = out.shape[0]
-        total = v[0, 0:pixels, :].astype(F32)
-        for d in range(1, pairs):
-            total = total + v[d, 0:pixels, :].astype(F32)
-        v[pairs, 0:pixels, :] = total.astype(BF16)
-        stores.append(start(v.at[pairs, 0:pixels, :], out, sem_out.at[n]))
+    pieces, (fine_out, coarse_out, out, held, sem_in, sem_out) = rest[:pairs], rest[pairs:]
+    loads = [start(pieces[d], held.at[d], sem_in.at[d]) for d in range(pairs)]
+    for load in loads:
+        load.wait()
+    pixels = out.shape[0]
+    total = held[0, 0:pixels, :].astype(F32)
+    for d in range(1, pairs):
+        total = total + held[d, 0:pixels, :].astype(F32)
+    held[pairs, 0:pixels, :] = total.astype(BF16)
+    store = start(held.at[pairs, 0:pixels, :], out, sem_out)
     total = mine[...]
     for d in range(1, pairs):
-        total = total + from_pair(v_coarse[d, pixels:, :])
-    for lane0, row, out in ((0, fine_row, fine_out), (banks, coarse_row, coarse_out)):
+        total = total + from_pair(held[d, pixels:, :])
+    for lane0, row, logit in ((0, fine_row, fine_out), (banks, coarse_row, coarse_out)):
         own = row[:, 0:banks]
         some = total[0:1, lane0 : lane0 + banks]
-        out[...] = own * (some - jnp.sum(own * some, axis=1, keepdims=True))
-    for store in stores:
-        store.wait()
+        logit[...] = own * (some - jnp.sum(own * some, axis=1, keepdims=True))
+    store.wait()
 
 
 def shape(*dims, dtype=BF16):
@@ -552,11 +553,11 @@
             pltpu.VMEM((coarse_px, channels), BF16), pltpu.VMEM((coarse_px, width), BF16),
             dma((2,)), dma((2, pairs)),
         ],
-        nbytes=bank_bytes, alone=True,
+        nbytes=bank_bytes, grant=67043328,
     )(cx, cup)
     bufs = to_pairs(packs)
     chunk = chunk_of(rows, count)
-    fine_sum, fine_row, coarse_sum, coarse_row = call(
+    fine_table, fine_row, coarse_table, coarse_row = call(
         functools.partial(tables_body, pairs, chunk),
         [shape(2 * banks * chunk, count * chunk), shape(1, 128, dtype=F32)] * 2,
         smem(2), vmem(4), flops=work, nbytes=bank_bytes,
@@ -566,7 +567,7 @@
         functools.partial(mix_body, pairs),
         [shape(block, span)] * pairs, hbm(3), hbm(pairs),
         mix_scratch() + [dma, dma((2, taps)), dma((pairs, taps))],
-        flops=4 * banks * pairs * block * span, nbytes=3 * bank_bytes,
+        flops=4 * banks * pairs * block * span, nbytes=3 * bank_bytes, grant=65500000,
     )(fc, fb, other_fb)
     mixed = to_pairs(mixed)
 
@@ -663,19 +664,22 @@
             flops=2 * banks * count * rows * span, nbytes=3 * bank_bytes,
         )(table, *own, *others)[0]
 
-    fine_update = update(fine_sum, fine_own, swapped[0])
-    coarse_update = update(coarse_sum, coarse_own, swapped[1])
-
-    fine_logit, coarse_logit, fine_delta, coarse_delta = call(
+    fine_update = update(fine_table, fine_own, swapped[0])
+    coarse_update = update(coarse_table, coarse_own, swapped[1])
+
+    fine_delta = call(
+        functools.partial(sum_body, pairs),
+        shape(fine_px, block), hbm(pairs), hbm(1)[0],
+        [pltpu.VMEM((pairs + 1, fine_px, block), BF16), dma((pairs,)), dma],
+        nbytes=2 * fine_px * channels,
+    )(*fine_parts)
+    fine_logit, coarse_logit, coarse_delta = call(
         functools.partial(final_body, pairs, banks),
-        [shape(1, banks, dtype=F32)] * 2 + [shape(fine_px, block), shape(coarse_px, block)],
-        vmem(3) + hbm(2 * pairs), vmem(2) + hbm(2),
-        [
-            pltpu.VMEM((pairs + 1, fine_px, block), BF16),
-            pltpu.VMEM((pairs + 1, coarse_px + 16, block), BF16), dma((2, pairs)), dma((2,)),
-        ],
-        nbytes=2 * fine_px * channels,
-    )(mine, fine_row, coarse_row, *fine_parts, *slots)
+        [shape(1, banks, dtype=F32)] * 2 + [shape(coarse_px, block)],
+        vmem(3) + hbm(pairs), vmem(2) + hbm(1),
+        [pltpu.VMEM((pairs + 1, coarse_px + 16, block), BF16), dma((pairs,)), dma],
+        nbytes=2 * coarse_px * channels,
+    )(mine, fine_row, coarse_row, *slots)
     fine_delta = fine_delta.reshape(1, fine_side, fine_side, block)
     coarse_delta = coarse_delta.reshape(1, coarse_side, coarse_side, block)
     return (fine_delta, fine_update, fine_logit, coarse_delta, coarse_update, coarse_logit)

time: 96.2 us -> 99.5 us (1.034)
  the two profiles are of different devices: /device:TPU:0 before, /device:TPU:10 now
where the time goes in v1:
time: 99.5 us; the launch traced here: 98.8 us
  Pallas kernels  34.2 us (34%)
  waiting for transfers between devices  31.3 us (31%)
  starting transfers between devices  24.7 us (25%)
  local copies, waits for them, and re-layouts  7.56 us (8%)
    ppermute x6, waiting for transfers between devices, over_chan(): return lax.ppermute(x, 'chan', [(i, i ^ d) for i in range(pairs)])  16.2 us
    ppermute x22, starting transfers between devices, over_batch(): return lax.ppermute(x, 'batch', [(i, i ^ d) for i in range(count)])  16.1 us
    ppermute x22, waiting for transfers between devices, over_batch(): return lax.ppermute(x, 'batch', [(i, i ^ d) for i in range(count)])  15.1 us
    ppermute x6, starting transfers between devices, over_chan(): return lax.ppermute(x, 'chan', [(i, i ^ d) for i in range(pairs)])  8.62 us
    pallas_call x2, Pallas kernels, update(): call(functools.partial(update_body, pairs, 1), [shape(banks, taps, rows,...  7.7 us
    unnamed x52, local copies, waits for them, and re-layouts  7.56 us
    pallas_call x1, Pallas kernels, pair_steps(): call(functools.partial(coarse_body, pairs, coarse_side), [shape(coarse_px...  4.84 us
    pallas_call x1, Pallas kernels, pair_steps(): call(functools.partial(mix_body, pairs), [shape(block, span)] * pairs, hb...  3.6 us
  transfers between devices with their start and end apart: 28, of which 9 were waited for; matrix products, arithmetic and copies ran while one was open for 0% of the time, Pallas kernels for 34%

profile of v1, /device:TPU:10, one launch (start us, length us, event | category | flops | bytes accessed | tf_op | source)
XLA Modules:
  0.0 98.8 jit_solution(18235768782438668441)
XLA Ops:
  1.2 1.8 %shard_map.133 = (bf16[512,128]{1,0:T(8,128)(2,1)}, bf16[512,128]{1,0:T(8,128)(2,1)}, bf16[512,128]{1,0:T(8,128)(2,1)}, bf16[512,128]{1,0:T(8,128)(2,1)}) custom-call(bf16[256,512]{1,0:T(8,128)(2,1)} %bitcast.10, bf16[256,128]{1,0:T(8,128)(2,1)} %bitcast.11), custom_call_target="tpu_custom_call" | custom-call | bytes 1179648 | tf_op jit(solution)/shard_map/pallas_call | solution.py:549
  3.0 0.6 collective-permute-start.15
  3.6 1.5 %collective-permute-start.16 = (bf16[512,128]{1,0:T(8,128)(2,1)}, bf16[512,128]{1,0:T(8,128)(2,1)S(1)}, u32[]{:S(2)}, u32[]{:S(2)}) collective-permute-start(bf16[512,128]{1,0:T(8,128)(2,1)} %get-tuple-element.62), channel_id=1, source_target_pairs={{0,16},{4,20},{8,24},{12,28},{16,0},{20,4},{24,8},{28,12},{1,17},{... | collective-permute-start | bytes 393224 | tf_op jit(solution)/shard_map/ppermute | solution.py:525
  5.1 1.4 %collective-permute-start.17 = (bf16[512,128]{1,0:T(8,128)(2,1)}, bf16[512,128]{1,0:T(8,128)(2,1)S(1)}, u32[]{:S(2)}, u32[]{:S(2)}) collective-permute-start(bf16[512,128]{1,0:T(8,128)(2,1)} %get-tuple-element.63), channel_id=1, source_target_pairs={{0,24},{4,28},{8,16},{12,20},{16,8},{20,12},{24,0},{28,4},{1,25},{... | collective-permute-start | bytes 393224 | tf_op jit(solution)/shard_map/ppermute | solution.py:525
  6.5 1.2 %copy-done.19 = bf16[1,32,32,512]{3,2,1,0:T(8,128)(2,1)S(1)} copy-done((bf16[1,32,32,512]{3,2,1,0:T(8,128)(2,1)S(1)}, bf16[1,32,32,512]{3,2,1,0:T(8,128)(2,1)}, u32[]{:S(2)}) %copy-start.19) | copy-done | bytes 1048600
  7.8 0.9 copy-done.21
  8.7 2.1 %shard_map.131 = (bf16[128,1152]{1,0:T(8,128)(2,1)S(1)}, bf16[128,1152]{1,0:T(8,128)(2,1)S(1)}, bf16[128,1152]{1,0:T(8,128)(2,1)S(1)}, bf16[128,1152]{1,0:T(8,128)(2,1)S(1)}) custom-call(bf16[1024,512]{1,0:T(8,128)(2,1)S(1)} %bitcast.6, bf16[1024,128]{1,0:T(8,128)(2,1)S(1)} %bitcast.7), custom_call_target="tpu_custom_call" | custom-call | flops 1207959552 | bytes 2621440 | tf_op jit(solution)/shard_map/pallas_call | solution.py:586
  10.9 0.6 collective-permute-start.7
  11.5 1.8 %collective-permute-start.8 = (bf16[128,1152]{1,0:T(8,128)(2,1)S(1)}, bf16[128,1152]{1,0:T(8,128)(2,1)}, u32[]{:S(2)}, u32[]{:S(2)}) collective-permute-start(bf16[128,1152]{1,0:T(8,128)(2,1)S(1)} %get-tuple-element.58), channel_id=1, source_target_pairs={{0,16},{4,20},{8,24},{12,28},{16,0},{20,4},{24,8},{28,12},{1,17},{... | collective-permute-start | bytes 884744 | tf_op jit(solution)/shard_map/ppermute | solution.py:525
  13.3 1.4 %collective-permute-start.9 = (bf16[128,1152]{1,0:T(8,128)(2,1)S(1)}, bf16[128,1152]{1,0:T(8,128)(2,1)}, u32[]{:S(2)}, u32[]{:S(2)}) collective-permute-start(bf16[128,1152]{1,0:T(8,128)(2,1)S(1)} %get-tuple-element.59), channel_id=1, source_target_pairs={{0,24},{4,28},{8,16},{12,20},{16,8},{20,12},{24,0},{28,4},{1,25},{... | collective-permute-start | bytes 884744 | tf_op jit(solution)/shard_map/ppermute | solution.py:525
  14.8 6.1 %collective-permute-done.7.rest_2_.rest_1_ = bf16[128,1152]{1,0:T(8,128)(2,1)S(1)} collective-permute-done((bf16[128,1152]{1,0:T(8,128)(2,1)S(1)}, bf16[128,1152]{1,0:T(8,128)(2,1)S(1)}, u32[]{:S(2)}, u32[]{:S(2)}) %collective-permute-start.7) | collective-permute-done | bytes 294944 | tf_op jit(solution)/shard_map/ppermute | solution.py:525
  20.8 3.9 %collective-permute-done.8.rest_3_.rest_2_ = bf16[128,1152]{1,0:T(8,128)(2,1)} collective-permute-done((bf16[128,1152]{1,0:T(8,128)(2,1)S(1)}, bf16[128,1152]{1,0:T(8,128)(2,1)}, u32[]{:S(2)}, u32[]{:S(2)}) %collective-permute-start.8) | collective-permute-done | bytes 294944 | tf_op jit(solution)/shard_map/ppermute | solution.py:525
  24.7 1.7 %collective-permute-done.9.rest_4_.rest_3_ = bf16[128,1152]{1,0:T(8,128)(2,1)} collective-permute-done((bf16[128,1152]{1,0:T(8,128)(2,1)S(1)}, bf16[128,1152]{1,0:T(8,128)(2,1)}, u32[]{:S(2)}, u32[]{:S(2)}) %collective-permute-start.9) | collective-permute-done | bytes 294944 | tf_op jit(solution)/shard_map/ppermute | solution.py:525
  27.0 3.6 %shard_map.135 = (bf16[128,1152]{1,0:T(8,128)(2,1)S(1)}, bf16[128,1152]{1,0:T(8,128)(2,1)S(1)}, bf16[128,1152]{1,0:T(8,128)(2,1)S(1)}, bf16[128,1152]{1,0:T(8,128)(2,1)S(1)}, f32[4,128]{1,0:T(4,128)S(1)}) custom-call(bf16[8,9,64,128]{3,2,1,0:T(8,128)(2,1)S(1)} %copy-done.18, bf16[8,9,64,128]{3,2,1,0:T(8,128)(2,1)} %collective-permute-done.14.other, ...), custom_call_target="tpu_custom_call" | custom-call | flops 1207959552 | bytes 3538944 | tf_op jit(solution)/shard_map/pallas_call | solution.py:613
  30.6 0.7 copy-done.5
  31.3 4.8 %shard_map.134 = (bf16[256,128]{1,0:T(8,128)(2,1)S(1)}, bf16[256,128]{1,0:T(8,128)(2,1)S(1)}, bf16[256,128]{1,0:T(8,128)(2,1)S(1)}, bf16[256,128]{1,0:T(8,128)(2,1)S(1)}) custom-call(f32[8,8]{1,0:T(8,128)S(1)} %copy-done.24, bf16[8,9,64,128]{3,2,1,0:T(8,128)(2,1)S(1)} %copy-done.18, bf16[8,9,64,128]{3,2,1,0:T(8,128)(2,1)} %collective-permute-done.14.other, ...), custom_call_target="tpu_custom_call" | custom-call | flops 1207959552 | bytes 3538944 | tf_op jit(solution)/shard_map/pallas_call | solution.py:574
  36.2 3.4 %shard_map.136 = (bf16[272,128]{1,0:T(8,128)(2,1)}, bf16[272,128]{1,0:T(8,128)(2,1)}, bf16[272,128]{1,0:T(8,128)(2,1)}, f32[8,128]{1,0:T(8,128)S(1)}) custom-call(bf16[8,9,64,128]{3,2,1,0:T(8,128)(2,1)S(1)} %copy-done, bf16[8,9,64,128]{3,2,1,0:T(8,128)(2,1)} %collective-permute-done.other, f32[4,128]{1,0:T(4,128)S(1)} %get-tuple-element.65.more, ...), custom_call_target="tpu_custom_call" | custom-call | flops 1207959552 | bytes 3538944 | tf_op jit(solution)/shard_map/pallas_call | solution.py:627
  39.6 0.6 copy-done.16
  40.2 1.0 collective-permute-start.18
  41.2 0.7 copy-done.3
  41.9 1.7 %collective-permute-start.19 = (bf16[272,128]{1,0:T(8,128)(2,1)}, bf16[272,128]{1,0:T(8,128)(2,1)}, u32[]{:S(2)}, u32[]{:S(2)}) collective-permute-start(bf16[272,128]{1,0:T(8,128)(2,1)} %get-tuple-element.71), channel_id=1, source_target_pairs={{0,16},{4,20},{8,24},{12,28},{16,0},{20,4},{24,8},{28,12},{1,17},{... | collective-permute-start | bytes 208904 | tf_op jit(solution)/shard_map/ppermute | solution.py:525
  43.7 0.7 copy-done.13
  44.4 0.8 collective-permute-start.20
  45.2 3.6 %shard_map.127 = (bf16[128,1152]{1,0:T(8,128)(2,1)}, bf16[128,1152]{1,0:T(8,128)(2,1)}, bf16[128,1152]{1,0:T(8,128)(2,1)}, bf16[128,1152]{1,0:T(8,128)(2,1)}) custom-call(f32[8,8]{1,0:T(8,128)} %fine_coefs.1, bf16[8,9,64,128]{3,2,1,0:T(8,128)(2,1)} %own.7, bf16[8,9,64,128]{3,2,1,0:T(8,128)(2,1)} %collective-permute-done.other), custom_call_target="tpu_custom_call" | custom-call | flops 18874368 | bytes 3538944 | tf_op jit(solution)/shard_map/pallas_call | solution.py:566
  48.8 1.0 %collective-permute-start.1 = (bf16[128,1152]{1,0:T(8,128)(2,1)}, bf16[128,1152]{1,0:T(8,128)(2,1)S(1)}, u32[]{:S(2)}, u32[]{:S(2)}) collective-permute-start(bf16[128,1152]{1,0:T(8,128)(2,1)} %get-tuple-element.48), channel_id=1, source_target_pairs={{0,8},{4,12},{8,0},{12,4},{16,24},{20,28},{24,16},{28,20},{1,9},{5... | collective-permute-start | bytes 884744 | tf_op jit(solution)/shard_map/ppermute | solution.py:525
  49.9 1.7 %collective-permute-start.2 = (bf16[128,1152]{1,0:T(8,128)(2,1)}, bf16[128,1152]{1,0:T(8,128)(2,1)S(1)}, u32[]{:S(2)}, u32[]{:S(2)}) collective-permute-start(bf16[128,1152]{1,0:T(8,128)(2,1)} %get-tuple-element.49), channel_id=1, source_target_pairs={{0,16},{4,20},{8,24},{12,28},{16,0},{20,4},{24,8},{28,12},{1,17},{... | collective-permute-start | bytes 884744 | tf_op jit(solution)/shard_map/ppermute | solution.py:525
  51.6 0.8 collective-permute-start.3
  52.4 0.7 copy-done.17
  53.1 1.4 %shard_map.137 = (bf16[272,128]{1,0:T(8,128)(2,1)S(1)}, bf16[272,128]{1,0:T(8,128)(2,1)S(1)}, bf16[272,128]{1,0:T(8,128)(2,1)S(1)}, bf16[272,128]{1,0:T(8,128)(2,1)S(1)}, f32[8,128]{1,0:T(8,128)S(1)}) custom-call(bf16[256,128]{1,0:T(8,128)(2,1)S(1)} %get-tuple-element.64.first_part, f32[8,128]{1,0:T(8,128)S(1)} %copy-done.17, ...), custom_call_target="tpu_custom_call" | custom-call | bytes 524288 | tf_op jit(solution)/shard_map/pallas_call | solution.py:640
  54.6 0.5 collective-permute-start.21
  55.1 2.6 %collective-permute-start.22 = (bf16[272,128]{1,0:T(8,128)(2,1)S(1)}, bf16[272,128]{1,0:T(8,128)(2,1)S(1)}, u32[]{:S(2)}, u32[]{:S(2)}) collective-permute-start(bf16[272,128]{1,0:T(8,128)(2,1)S(1)} %get-tuple-element.78), channel_id=1, source_target_pairs={{0,2},{1,3},{2,0},{3,1},{4,6},{5,7},{6,4},{7,5},{8,10},{9,11},{10,... | collective-permute-start | bytes 208904 | tf_op jit(solution)/shard_map/ppermute | solution.py:528
  57.7 1.8 %collective-permute-done.21.rest_1_ = bf16[272,128]{1,0:T(8,128)(2,1)S(1)} collective-permute-done((bf16[272,128]{1,0:T(8,128)(2,1)S(1)}, bf16[272,128]{1,0:T(8,128)(2,1)S(1)}, u32[]{:S(2)}, u32[]{:S(2)}) %collective-permute-start.21) | collective-permute-done | bytes 69664 | tf_op jit(solution)/shard_map/ppermute | solution.py:528
  59.5 1.3 %collective-permute-done.22.rest_2_ = bf16[272,128]{1,0:T(8,128)(2,1)S(1)} collective-permute-done((bf16[272,128]{1,0:T(8,128)(2,1)S(1)}, bf16[272,128]{1,0:T(8,128)(2,1)S(1)}, u32[]{:S(2)}, u32[]{:S(2)}) %collective-permute-start.22) | collective-permute-done | bytes 69664 | tf_op jit(solution)/shard_map/ppermute | solution.py:528
  61.3 3.4 %collective-permute-done.2.rest_2_ = bf16[128,1152]{1,0:T(8,128)(2,1)S(1)} collective-permute-done((bf16[128,1152]{1,0:T(8,128)(2,1)}, bf16[128,1152]{1,0:T(8,128)(2,1)S(1)}, u32[]{:S(2)}, u32[]{:S(2)}) %collective-permute-start.2) | collective-permute-done | bytes 294944 | tf_op jit(solution)/shard_map/ppermute | solution.py:525
  64.7 1.6 %collective-permute-start.23 = (bf16[272,128]{1,0:T(8,128)(2,1)S(1)}, bf16[272,128]{1,0:T(8,128)(2,1)S(1)}, u32[]{:S(2)}, u32[]{:S(2)}) collective-permute-start(bf16[272,128]{1,0:T(8,128)(2,1)S(1)} %get-tuple-element.79), channel_id=1, source_target_pairs={{0,3},{1,2},{2,1},{3,0},{4,7},{5,6},{6,5},{7,4},{8,11},{9,10},{10,... | collective-permute-start | bytes 208904 | tf_op jit(solution)/shard_map/ppermute | solution.py:528
  66.3 1.0 copy-done.20
  67.3 0.9 copy-done.22
  68.2 2.3 %shard_map.128 = (bf16[1024,128]{1,0:T(8,128)(2,1)S(1)}, bf16[1024,128]{1,0:T(8,128)(2,1)S(1)}, bf16[1024,128]{1,0:T(8,128)(2,1)S(1)}, bf16[1024,128]{1,0:T(8,128)(2,1)S(1)}) custom-call(bf16[1024,128]{1,0:T(8,128)(2,1)S(1)} %bitcast.8, bf16[128,1152]{1,0:T(8,128)(2,1)S(1)} %copy-done.20, bf16[128,1152]{1,0:T(8,128)(2,1)S(1)} %collective-permute-done.1.rest_1_, ...), custom_call_target="tpu_custom_call" | custom-call | flops 1207959552 | bytes 2621440 | tf_op jit(solution)/shard_map/pallas_call | solution.py:598
  70.8 2.3 %collective-permute-start.4 = (bf16[1024,128]{1,0:T(8,128)(2,1)S(1)}, bf16[1024,128]{1,0:T(8,128)(2,1)S(1)}, u32[]{:S(2)}, u32[]{:S(2)}) collective-permute-start(bf16[1024,128]{1,0:T(8,128)(2,1)S(1)} %get-tuple-element.52), channel_id=1, source_target_pairs={{0,1},{1,0},{2,3},{3,2},{4,5},{5,4},{6,7},{7,6},{8,9},{9,8},{10,11... | collective-permute-start | bytes 786440 | tf_op jit(solution)/shard_map/ppermute | solution.py:528
  73.0 0.6 collective-permute-start.5
  73.7 1.0 %collective-permute-start.6 = (bf16[1024,128]{1,0:T(8,128)(2,1)S(1)}, bf16[1024,128]{1,0:T(8,128)(2,1)S(1)}, u32[]{:S(2)}, u32[]{:S(2)}) collective-permute-start(bf16[1024,128]{1,0:T(8,128)(2,1)S(1)} %get-tuple-element.54), channel_id=1, source_target_pairs={{0,3},{1,2},{2,1},{3,0},{4,7},{5,6},{6,5},{7,4},{8,11},{9,10},{10,... | collective-permute-start | bytes 786440 | tf_op jit(solution)/shard_map/ppermute | solution.py:528
  74.7 0.8 shard_map.130
  75.5 4.0 %shard_map.132 = f32[8,9,64,128]{3,2,1,0:T(8,128)} custom-call(bf16[512,256]{1,0:T(8,128)(2,1)S(1)} %get-tuple-element.55.rest_0_, bf16[128,1152]{1,0:T(8,128)(2,1)S(1)} %get-tuple-element.56.rest_1_.rest_0_, bf16[128,1152]{1,0:T(8,128)(2,1)S(1)} %copy-done.2, bf16[128,1152]{1,0:T(8,128)(2,1)} %collective-permute-done.8.rest_3_.rest_2_, ...), custom_call_target="tpu_custom_call" | custom-call | flops 9437184 | bytes 3538944 | tf_op jit(solution)/shard_map/pallas_call | solution.py:656
  79.5 1.7 %shard_map.138 = (f32[1,8]{1,0:T(1,128)}, f32[1,8]{1,0:T(1,128)}, bf16[256,128]{1,0:T(8,128)(2,1)}) custom-call(f32[8,128]{1,0:T(8,128)S(1)} %get-tuple-element.73.mine, f32[1,128]{1,0:T(1,128)S(1)} %get-tuple-element.74.fine_row, f32[1,128]{1,0:T(1,128)S(1)} %get-tuple-element.75.coarse_row, bf16[272,128]{1,0:T(8,128)(2,1)S(1)} %get-tuple-element.76.rest_0_, ...), custom_call_target="tpu_custom_call" | custom-call | bytes 262144 | tf_op jit(solution)/shard_map/pallas_call | solution.py:676
  81.3 3.7 %shard_map.139 = f32[8,9,64,128]{3,2,1,0:T(8,128)} custom-call(bf16[512,256]{1,0:T(8,128)(2,1)S(1)} %get-tuple-element.82.rest_0_, bf16[128,1152]{1,0:T(8,128)(2,1)S(1)} %copy-done.6, bf16[128,1152]{1,0:T(8,128)(2,1)S(1)} %copy-done.8, bf16[128,1152]{1,0:T(8,128)(2,1)S(1)} %copy-done.10, bf16[128,1152]{1,0:T(8,128)(2,1)S(1)} %copy-done.12, ...), custom_call_target="tpu_custom_call" | custom-call | flops 9437184 | bytes 3538944 | tf_op jit(solution)/shard_map/pallas_call | solution.py:656
  85.0 6.6 %collective-permute-done.5.rest_2_ = bf16[1024,128]{1,0:T(8,128)(2,1)S(1)} collective-permute-done((bf16[1024,128]{1,0:T(8,128)(2,1)S(1)}, bf16[1024,128]{1,0:T(8,128)(2,1)S(1)}, u32[]{:S(2)}, u32[]{:S(2)}) %collective-permute-start.5) | collective-permute-done | bytes 262176 | tf_op jit(solution)/shard_map/ppermute | solution.py:528
  91.6 6.2 %collective-permute-done.6.rest_3_ = bf16[1024,128]{1,0:T(8,128)(2,1)S(1)} collective-permute-done((bf16[1024,128]{1,0:T(8,128)(2,1)S(1)}, bf16[1024,128]{1,0:T(8,128)(2,1)S(1)}, u32[]{:S(2)}, u32[]{:S(2)}) %collective-permute-start.6) | collective-permute-done | bytes 262176 | tf_op jit(solution)/shard_map/ppermute | solution.py:528
  97.8 1.0 shard_map.129
  (73 shorter events, 2.0 us)
Async XLA Ops:
  0.6 25.8 %collective-permute-start.14 = (bf16[8,9,64,128]{3,2,1,0:T(8,128)(2,1)}, bf16[8,9,64,128]{3,2,1,0:T(8,128)(2,1)}, u32[]{:S(2)}, u32[]{:S(2)}) collective-permute-start(bf16[8,9,64,128]{3,2,1,0:T(8,128)(2,1)} %own.6), channel_id=1, source_target_pairs={{0,4},{4,0},{8,12},{12,8},{16,20},{20,16},{24,28},{28,24},{1,5},{5... | collective-permute-start | bytes 3538952 | tf_op jit(solution)/shard_map/ppermute | solution.py:525
  0.7 35.5 %collective-permute-start = (bf16[8,9,64,128]{3,2,1,0:T(8,128)(2,1)}, bf16[8,9,64,128]{3,2,1,0:T(8,128)(2,1)}, u32[]{:S(2)}, u32[]{:S(2)}) collective-permute-start(bf16[8,9,64,128]{3,2,1,0:T(8,128)(2,1)} %own.7), channel_id=1, source_target_pairs={{0,4},{4,0},{8,12},{12,8},{16,20},{20,16},{24,28},{28,24},{1,5},{5... | collective-permute-start | bytes 3538952 | tf_op jit(solution)/shard_map/ppermute | solution.py:525
  3.0 7.9 %collective-permute-start.15 = (bf16[512,128]{1,0:T(8,128)(2,1)}, bf16[512,128]{1,0:T(8,128)(2,1)S(1)}, u32[]{:S(2)}, u32[]{:S(2)}) collective-permute-start(bf16[512,128]{1,0:T(8,128)(2,1)} %get-tuple-element.61), channel_id=1, source_target_pairs={{0,8},{4,12},{8,0},{12,4},{16,24},{20,28},{24,16},{28,20},{1,9},{5... | collective-permute-start | bytes 393224 | tf_op jit(solution)/shard_map/ppermute | solution.py:525
  3.6 7.9 %collective-permute-start.16 = (bf16[512,128]{1,0:T(8,128)(2,1)}, bf16[512,128]{1,0:T(8,128)(2,1)S(1)}, u32[]{:S(2)}, u32[]{:S(2)}) collective-permute-start(bf16[512,128]{1,0:T(8,128)(2,1)} %get-tuple-element.62), channel_id=1, source_target_pairs={{0,16},{4,20},{8,24},{12,28},{16,0},{20,4},{24,8},{28,12},{1,17},{... | collective-permute-start | bytes 393224 | tf_op jit(solution)/shard_map/ppermute | solution.py:525
  5.1 8.2 %collective-permute-start.17 = (bf16[512,128]{1,0:T(8,128)(2,1)}, bf16[512,128]{1,0:T(8,128)(2,1)S(1)}, u32[]{:S(2)}, u32[]{:S(2)}) collective-permute-start(bf16[512,128]{1,0:T(8,128)(2,1)} %get-tuple-element.63), channel_id=1, source_target_pairs={{0,24},{4,28},{8,16},{12,20},{16,8},{20,12},{24,0},{28,4},{1,25},{... | collective-permute-start | bytes 393224 | tf_op jit(solution)/shard_map/ppermute | solution.py:525
  6.5 1.2 %copy-start.19 = (bf16[1,32,32,512]{3,2,1,0:T(8,128)(2,1)S(1)}, bf16[1,32,32,512]{3,2,1,0:T(8,128)(2,1)}, u32[]{:S(2)}) copy-start(bf16[1,32,32,512]{3,2,1,0:T(8,128)(2,1)} %param.8) | copy-start | bytes 3145732
  7.8 0.9 copy-start.21
  8.7 18.3 %copy-start.18 = (bf16[8,9,64,128]{3,2,1,0:T(8,128)(2,1)S(1)}, bf16[8,9,64,128]{3,2,1,0:T(8,128)(2,1)}, u32[]{:S(2)}) copy-start(bf16[8,9,64,128]{3,2,1,0:T(8,128)(2,1)} %own.6) | copy-start | bytes 3538948
  8.7 18.3 %copy-start.23 = (bf16[512,128]{1,0:T(8,128)(2,1)S(1)}, bf16[512,128]{1,0:T(8,128)(2,1)}, u32[]{:S(2)}) copy-start(bf16[512,128]{1,0:T(8,128)(2,1)} %get-tuple-element.60.rest_0_) | copy-start | bytes 393220
  10.9 9.9 %collective-permute-start.7 = (bf16[128,1152]{1,0:T(8,128)(2,1)S(1)}, bf16[128,1152]{1,0:T(8,128)(2,1)S(1)}, u32[]{:S(2)}, u32[]{:S(2)}) collective-permute-start(bf16[128,1152]{1,0:T(8,128)(2,1)S(1)} %get-tuple-element.57), channel_id=1, source_target_pairs={{0,8},{4,12},{8,0},{12,4},{16,24},{20,28},{24,16},{28,20},{1,9},{5... | collective-permute-start | bytes 884744 | tf_op jit(solution)/shard_map/ppermute | solution.py:525
  11.5 13.3 %collective-permute-start.8 = (bf16[128,1152]{1,0:T(8,128)(2,1)S(1)}, bf16[128,1152]{1,0:T(8,128)(2,1)}, u32[]{:S(2)}, u32[]{:S(2)}) collective-permute-start(bf16[128,1152]{1,0:T(8,128)(2,1)S(1)} %get-tuple-element.58), channel_id=1, source_target_pairs={{0,16},{4,20},{8,24},{12,28},{16,0},{20,4},{24,8},{28,12},{1,17},{... | collective-permute-start | bytes 884744 | tf_op jit(solution)/shard_map/ppermute | solution.py:525
  13.3 13.2 %collective-permute-start.9 = (bf16[128,1152]{1,0:T(8,128)(2,1)S(1)}, bf16[128,1152]{1,0:T(8,128)(2,1)}, u32[]{:S(2)}, u32[]{:S(2)}) collective-permute-start(bf16[128,1152]{1,0:T(8,128)(2,1)S(1)} %get-tuple-element.59), channel_id=1, source_target_pairs={{0,24},{4,28},{8,16},{12,20},{16,8},{20,12},{24,0},{28,4},{1,25},{... | collective-permute-start | bytes 884744 | tf_op jit(solution)/shard_map/ppermute | solution.py:525
  20.8 15.4 %copy-start.1 = (bf16[128,1152]{1,0:T(8,128)(2,1)}, bf16[128,1152]{1,0:T(8,128)(2,1)S(1)}, u32[]{:S(2)}) copy-start(bf16[128,1152]{1,0:T(8,128)(2,1)S(1)} %collective-permute-done.7.rest_2_.rest_1_) | copy-start | bytes 884740
  20.8 20.4 %collective-permute-start.10 = (bf16[128,1152]{1,0:T(8,128)(2,1)S(1)}, bf16[128,1152]{1,0:T(8,128)(2,1)S(1)}, u32[]{:S(2)}, u32[]{:S(2)}) collective-permute-start(bf16[128,1152]{1,0:T(8,128)(2,1)S(1)} %get-tuple-element.56.rest_1_.rest_0_), channel_id=1, source_target_pairs={{0,4},{4,0},{8,12},{12,8},{16,20},{20,16},{24,28},{28,24},{1,5},{5... | collective-permute-start | bytes 884744 | tf_op jit(solution)/shard_map/ppermute | solution.py:525
  24.7 18.9 %collective-permute-start.11 = (bf16[128,1152]{1,0:T(8,128)(2,1)S(1)}, bf16[128,1152]{1,0:T(8,128)(2,1)S(1)}, u32[]{:S(2)}, u32[]{:S(2)}) collective-permute-start(bf16[128,1152]{1,0:T(8,128)(2,1)S(1)} %collective-permute-done.7.rest_2_.rest_1_), channel_id=1, source_target_pairs={{0,4},{4,0},{8,12},{12,8},{16,20},{20,16},{24,28},{28,24},{1,5},{5... | collective-permute-start | bytes 884744 | tf_op jit(solution)/shard_map/ppermute | solution.py:525
  26.5 28.1 %collective-permute-start.12 = (bf16[128,1152]{1,0:T(8,128)(2,1)}, bf16[128,1152]{1,0:T(8,128)(2,1)}, u32[]{:S(2)}, u32[]{:S(2)}) collective-permute-start(bf16[128,1152]{1,0:T(8,128)(2,1)} %collective-permute-done.8.rest_3_.rest_2_), channel_id=1, source_target_pairs={{0,4},{4,0},{8,12},{12,8},{16,20},{20,16},{24,28},{28,24},{1,5},{5... | collective-permute-start | bytes 884744 | tf_op jit(solution)/shard_map/ppermute | solution.py:525
  26.5 28.6 %collective-permute-start.13 = (bf16[128,1152]{1,0:T(8,128)(2,1)}, bf16[128,1152]{1,0:T(8,128)(2,1)}, u32[]{:S(2)}, u32[]{:S(2)}) collective-permute-start(bf16[128,1152]{1,0:T(8,128)(2,1)} %collective-permute-done.9.rest_4_.rest_3_), channel_id=1, source_target_pairs={{0,4},{4,0},{8,12},{12,8},{16,20},{20,16},{24,28},{28,24},{1,5},{5... | collective-permute-start | bytes 884744 | tf_op jit(solution)/shard_map/ppermute | solution.py:525
  27.0 4.3 %copy-start.24 = (f32[8,8]{1,0:T(8,128)S(1)}, f32[8,8]{1,0:T(8,128)}, u32[]{:S(2)}) copy-start(f32[8,8]{1,0:T(8,128)} %coefs.3) | copy-start | bytes 772
  31.3 4.9 %copy-start.7 = (bf16[128,1152]{1,0:T(8,128)(2,1)}, bf16[128,1152]{1,0:T(8,128)(2,1)S(1)}, u32[]{:S(2)}) copy-start(bf16[128,1152]{1,0:T(8,128)(2,1)S(1)} %get-tuple-element.84.rest_2_) | copy-start | bytes 884740
  31.3 4.9 %copy-start.9 = (bf16[128,1152]{1,0:T(8,128)(2,1)}, bf16[128,1152]{1,0:T(8,128)(2,1)S(1)}, u32[]{:S(2)}) copy-start(bf16[128,1152]{1,0:T(8,128)(2,1)S(1)} %get-tuple-element.85.rest_3_) | copy-start | bytes 884740
  31.3 4.9 %copy-start.11 = (bf16[128,1152]{1,0:T(8,128)(2,1)}, bf16[128,1152]{1,0:T(8,128)(2,1)S(1)}, u32[]{:S(2)}) copy-start(bf16[128,1152]{1,0:T(8,128)(2,1)S(1)} %get-tuple-element.86.rest_4_) | copy-start | bytes 884740
  31.3 4.9 %copy-start = (bf16[8,9,64,128]{3,2,1,0:T(8,128)(2,1)S(1)}, bf16[8,9,64,128]{3,2,1,0:T(8,128)(2,1)}, u32[]{:S(2)}) copy-start(bf16[8,9,64,128]{3,2,1,0:T(8,128)(2,1)} %own.7) | copy-start | bytes 3538948
  40.2 8.6 %collective-permute-start.18 = (bf16[272,128]{1,0:T(8,128)(2,1)}, bf16[272,128]{1,0:T(8,128)(2,1)}, u32[]{:S(2)}, u32[]{:S(2)}) collective-permute-start(bf16[272,128]{1,0:T(8,128)(2,1)} %get-tuple-element.70), channel_id=1, source_target_pairs={{0,8},{4,12},{8,0},{12,4},{16,24},{20,28},{24,16},{28,20},{1,9},{5... | collective-permute-start | bytes 208904 | tf_op jit(solution)/shard_map/ppermute | solution.py:525
  41.9 8.0 %collective-permute-start.19 = (bf16[272,128]{1,0:T(8,128)(2,1)}, bf16[272,128]{1,0:T(8,128)(2,1)}, u32[]{:S(2)}, u32[]{:S(2)}) collective-permute-start(bf16[272,128]{1,0:T(8,128)(2,1)} %get-tuple-element.71), channel_id=1, source_target_pairs={{0,16},{4,20},{8,24},{12,28},{16,0},{20,4},{24,8},{28,12},{1,17},{... | collective-permute-start | bytes 208904 | tf_op jit(solution)/shard_map/ppermute | solution.py:525
  44.4 15.1 %copy-start.6 = (bf16[128,1152]{1,0:T(8,128)(2,1)S(1)}, bf16[128,1152]{1,0:T(8,128)(2,1)}, u32[]{:S(2)}) copy-start(bf16[128,1152]{1,0:T(8,128)(2,1)} %copy-done.5) | copy-start | bytes 884740
  44.4 16.4 %copy-start.8 = (bf16[128,1152]{1,0:T(8,128)(2,1)S(1)}, bf16[128,1152]{1,0:T(8,128)(2,1)}, u32[]{:S(2)}) copy-start(bf16[128,1152]{1,0:T(8,128)(2,1)} %copy-done.7) | copy-start | bytes 884740
  44.4 16.4 %copy-start.10 = (bf16[128,1152]{1,0:T(8,128)(2,1)S(1)}, bf16[128,1152]{1,0:T(8,128)(2,1)}, u32[]{:S(2)}) copy-start(bf16[128,1152]{1,0:T(8,128)(2,1)} %copy-done.9) | copy-start | bytes 884740
  44.4 20.3 %copy-start.12 = (bf16[128,1152]{1,0:T(8,128)(2,1)S(1)}, bf16[128,1152]{1,0:T(8,128)(2,1)}, u32[]{:S(2)}) copy-start(bf16[128,1152]{1,0:T(8,128)(2,1)} %copy-done.11) | copy-start | bytes 884740
  44.4 7.2 %collective-permute-start.20 = (bf16[272,128]{1,0:T(8,128)(2,1)}, bf16[272,128]{1,0:T(8,128)(2,1)}, u32[]{:S(2)}, u32[]{:S(2)}) collective-permute-start(bf16[272,128]{1,0:T(8,128)(2,1)} %get-tuple-element.72), channel_id=1, source_target_pairs={{0,24},{4,28},{8,16},{12,20},{16,8},{20,12},{24,0},{28,4},{1,25},{... | collective-permute-start | bytes 208904 | tf_op jit(solution)/shard_map/ppermute | solution.py:525
  48.8 12.0 %collective-permute-start.1 = (bf16[128,1152]{1,0:T(8,128)(2,1)}, bf16[128,1152]{1,0:T(8,128)(2,1)S(1)}, u32[]{:S(2)}, u32[]{:S(2)}) collective-permute-start(bf16[128,1152]{1,0:T(8,128)(2,1)} %get-tuple-element.48), channel_id=1, source_target_pairs={{0,8},{4,12},{8,0},{12,4},{16,24},{20,28},{24,16},{28,20},{1,9},{5... | collective-permute-start | bytes 884744 | tf_op jit(solution)/shard_map/ppermute | solution.py:525
  49.9 14.8 %collective-permute-start.2 = (bf16[128,1152]{1,0:T(8,128)(2,1)}, bf16[128,1152]{1,0:T(8,128)(2,1)S(1)}, u32[]{:S(2)}, u32[]{:S(2)}) collective-permute-start(bf16[128,1152]{1,0:T(8,128)(2,1)} %get-tuple-element.49), channel_id=1, source_target_pairs={{0,16},{4,20},{8,24},{12,28},{16,0},{20,4},{24,8},{28,12},{1,17},{... | collective-permute-start | bytes 884744 | tf_op jit(solution)/shard_map/ppermute | solution.py:525
  51.6 13.0 %collective-permute-start.3 = (bf16[128,1152]{1,0:T(8,128)(2,1)}, bf16[128,1152]{1,0:T(8,128)(2,1)S(1)}, u32[]{:S(2)}, u32[]{:S(2)}) collective-permute-start(bf16[128,1152]{1,0:T(8,128)(2,1)} %get-tuple-element.50), channel_id=1, source_target_pairs={{0,24},{4,28},{8,16},{12,20},{16,8},{20,12},{24,0},{28,4},{1,25},{... | collective-permute-start | bytes 884744 | tf_op jit(solution)/shard_map/ppermute | solution.py:525
  54.6 4.9 %collective-permute-start.21 = (bf16[272,128]{1,0:T(8,128)(2,1)S(1)}, bf16[272,128]{1,0:T(8,128)(2,1)S(1)}, u32[]{:S(2)}, u32[]{:S(2)}) collective-permute-start(bf16[272,128]{1,0:T(8,128)(2,1)S(1)} %get-tuple-element.77), channel_id=1, source_target_pairs={{0,1},{1,0},{2,3},{3,2},{4,5},{5,4},{6,7},{7,6},{8,9},{9,8},{10,11... | collective-permute-start | bytes 208904 | tf_op jit(solution)/shard_map/ppermute | solution.py:528
  55.1 5.7 %collective-permute-start.22 = (bf16[272,128]{1,0:T(8,128)(2,1)S(1)}, bf16[272,128]{1,0:T(8,128)(2,1)S(1)}, u32[]{:S(2)}, u32[]{:S(2)}) collective-permute-start(bf16[272,128]{1,0:T(8,128)(2,1)S(1)} %get-tuple-element.78), channel_id=1, source_target_pairs={{0,2},{1,3},{2,0},{3,1},{4,6},{5,7},{6,4},{7,5},{8,10},{9,11},{10,... | collective-permute-start | bytes 208904 | tf_op jit(solution)/shard_map/ppermute | solution.py:528
  59.4 13.6 %collective-permute-start.24 = (bf16[128,1152]{1,0:T(8,128)(2,1)S(1)}, bf16[128,1152]{1,0:T(8,128)(2,1)S(1)}, u32[]{:S(2)}, u32[]{:S(2)}) collective-permute-start(bf16[128,1152]{1,0:T(8,128)(2,1)S(1)} %copy-done.6), channel_id=1, source_target_pairs={{0,4},{4,0},{8,12},{12,8},{16,20},{20,16},{24,28},{28,24},{1,5},{5... | collective-permute-start | bytes 884744 | tf_op jit(solution)/shard_map/ppermute | solution.py:525
  60.8 12.9 %collective-permute-start.25 = (bf16[128,1152]{1,0:T(8,128)(2,1)S(1)}, bf16[128,1152]{1,0:T(8,128)(2,1)S(1)}, u32[]{:S(2)}, u32[]{:S(2)}) collective-permute-start(bf16[128,1152]{1,0:T(8,128)(2,1)S(1)} %copy-done.8), channel_id=1, source_target_pairs={{0,4},{4,0},{8,12},{12,8},{16,20},{20,16},{24,28},{28,24},{1,5},{5... | collective-permute-start | bytes 884744 | tf_op jit(solution)/shard_map/ppermute | solution.py:525
  60.8 20.5 %collective-permute-start.26 = (bf16[128,1152]{1,0:T(8,128)(2,1)S(1)}, bf16[128,1152]{1,0:T(8,128)(2,1)S(1)}, u32[]{:S(2)}, u32[]{:S(2)}) collective-permute-start(bf16[128,1152]{1,0:T(8,128)(2,1)S(1)} %copy-done.10), channel_id=1, source_target_pairs={{0,4},{4,0},{8,12},{12,8},{16,20},{20,16},{24,28},{28,24},{1,5},{5... | collective-permute-start | bytes 884744 | tf_op jit(solution)/shard_map/ppermute | solution.py:525
  64.7 16.6 %collective-permute-start.27 = (bf16[128,1152]{1,0:T(8,128)(2,1)S(1)}, bf16[128,1152]{1,0:T(8,128)(2,1)S(1)}, u32[]{:S(2)}, u32[]{:S(2)}) collective-permute-start(bf16[128,1152]{1,0:T(8,128)(2,1)S(1)} %copy-done.12), channel_id=1, source_target_pairs={{0,4},{4,0},{8,12},{12,8},{16,20},{20,16},{24,28},{28,24},{1,5},{5... | collective-permute-start | bytes 884744 | tf_op jit(solution)/shard_map/ppermute | solution.py:525
  64.7 6.1 %collective-permute-start.23 = (bf16[272,128]{1,0:T(8,128)(2,1)S(1)}, bf16[272,128]{1,0:T(8,128)(2,1)S(1)}, u32[]{:S(2)}, u32[]{:S(2)}) collective-permute-start(bf16[272,128]{1,0:T(8,128)(2,1)S(1)} %get-tuple-element.79), channel_id=1, source_target_pairs={{0,3},{1,2},{2,1},{3,0},{4,7},{5,6},{6,5},{7,4},{8,11},{9,10},{10,... | collective-permute-start | bytes 208904 | tf_op jit(solution)/shard_map/ppermute | solution.py:528
  66.3 1.0 copy-start.20
  68.2 6.5 %copy-start.15 = (f32[8,8]{1,0:T(8,128)S(1)}, f32[8,8]{1,0:T(8,128)}, u32[]{:S(2)}) copy-start(f32[8,8]{1,0:T(8,128)} %fine_coefs.1) | copy-start | bytes 772
  68.2 6.5 %copy-start.25 = (f32[8,8]{1,0:T(8,128)S(1)}, f32[8,8]{1,0:T(8,128)}, u32[]{:S(2)}) copy-start(f32[8,8]{1,0:T(8,128)} %coefs.3) | copy-start | bytes 772
  70.8 14.2 %collective-permute-start.4 = (bf16[1024,128]{1,0:T(8,128)(2,1)S(1)}, bf16[1024,128]{1,0:T(8,128)(2,1)S(1)}, u32[]{:S(2)}, u32[]{:S(2)}) collective-permute-start(bf16[1024,128]{1,0:T(8,128)(2,1)S(1)} %get-tuple-element.52), channel_id=1, source_target_pairs={{0,1},{1,0},{2,3},{3,2},{4,5},{5,4},{6,7},{7,6},{8,9},{9,8},{10,11... | collective-permute-start | bytes 786440 | tf_op jit(solution)/shard_map/ppermute | solution.py:528
  73.0 18.5 %collective-permute-start.5 = (bf16[1024,128]{1,0:T(8,128)(2,1)S(1)}, bf16[1024,128]{1,0:T(8,128)(2,1)S(1)}, u32[]{:S(2)}, u32[]{:S(2)}) collective-permute-start(bf16[1024,128]{1,0:T(8,128)(2,1)S(1)} %get-tuple-element.53), channel_id=1, source_target_pairs={{0,2},{1,3},{2,0},{3,1},{4,6},{5,7},{6,4},{7,5},{8,10},{9,11},{10,... | collective-permute-start | bytes 786440 | tf_op jit(solution)/shard_map/ppermute | solution.py:528
  73.7 1.8 %copy-start.2 = (bf16[128,1152]{1,0:T(8,128)(2,1)S(1)}, bf16[128,1152]{1,0:T(8,128)(2,1)}, u32[]{:S(2)}) copy-start(bf16[128,1152]{1,0:T(8,128)(2,1)} %copy-done.1) | copy-start | bytes 884740
  73.7 1.8 %copy-start.4 = (bf16[128,1152]{1,0:T(8,128)(2,1)S(1)}, bf16[128,1152]{1,0:T(8,128)(2,1)}, u32[]{:S(2)}) copy-start(bf16[128,1152]{1,0:T(8,128)(2,1)} %copy-done.3) | copy-start | bytes 884740
  73.7 1.8 %copy-start.14 = (bf16[128,1152]{1,0:T(8,128)(2,1)S(1)}, bf16[128,1152]{1,0:T(8,128)(2,1)}, u32[]{:S(2)}) copy-start(bf16[128,1152]{1,0:T(8,128)(2,1)} %copy-done.13) | copy-start | bytes 884740
  73.7 24.2 %collective-permute-start.6 = (bf16[1024,128]{1,0:T(8,128)(2,1)S(1)}, bf16[1024,128]{1,0:T(8,128)(2,1)S(1)}, u32[]{:S(2)}, u32[]{:S(2)}) collective-permute-start(bf16[1024,128]{1,0:T(8,128)(2,1)S(1)} %get-tuple-element.54), channel_id=1, source_target_pairs={{0,3},{1,2},{2,1},{3,0},{4,7},{5,6},{6,5},{7,4},{8,11},{9,10},{10,... | collective-permute-start | bytes 786440 | tf_op jit(solution)/shard_map/ppermute | solution.py:528
  (6 other events, 4.4 us)
